TPU v7x, 1024 devices: a whole 8x8x8 slice. The times are simulated.
1024 devices in a mesh: seq: 32 (over y, z_lo), tp: 32 (over z_hi, x, core).
Axes of the slice: x: 8, y: 8, z: 8 (z_hi: 2, z_lo: 4; z = z_hi * 4 + z_lo), core: 2. Of those that a mesh axis runs over, the one named last changes fastest.
Arguments:
- lin_query: bfloat16 [8192, 64, 128], P('seq', 'tp'), may hold values from -6 to 6
- lin_key: bfloat16 [8192, 64, 128], P('seq', 'tp'), may hold values from -6 to 6
- lin_value: bfloat16 [8192, 64, 128], P('seq', 'tp'), may hold values from -80 to 80
- lin_gate: bfloat16 [8192, 64, 128], P('seq', 'tp'), may hold values from -6 to 6
- log_decay: float32 [8192, 64], P('seq', 'tp'), may hold values from -1 to 0
- norm_gain: float32 [64, 128], P('tp'), may hold values from 0.1 to 1.9
- doc_ids: int32 [8192], P('seq'), may hold values from 0 to 3, never falling along the last dimension, each value on 1 to 5120 neighbouring positions
- soft_query: bfloat16 [8192, 64, 128], P('seq', 'tp'), may hold values from -200 to 200
- soft_key: bfloat16 [8192, 8, 128], P('seq'), may hold values from -6 to 6
- soft_value: bfloat16 [8192, 8, 128], P('seq'), may hold values from -6 to 6
Outputs:
- lin_out: bfloat16 [8192, 64, 128], P('seq', 'tp')
- soft_out: bfloat16 [8192, 64, 128], P('seq', 'tp')
Inputs may be any that keep to these rules, and one draw needn't show every extreme that they name: `doc_ids`: ids never fall along the sequence; each document is one run of 1 to 5120 tokens, and one document has exactly that many.
All inputs are finite; a program needn't handle non-finite values.
Results may differ from a plain program's by a relative error of at most 0.012.
Values may be sent and summed in bfloat16 or wider, within the bound.
A program may use at most 32 MiB of HBM per device.

v0:
```python
import math

import jax
import jax.numpy as jnp
from jax import lax
from jax.sharding import Mesh
from jax.sharding import PartitionSpec as P

HEADS = 64
HEAD_DIM = 128
KV_HEADS = 8
SEQ = ("seq_0", "seq_1")


def filled_with(array, identity):
    return jax.tree.map(
        lambda part, zero: jnp.zeros_like(part) + jnp.asarray(zero, part.dtype), array, identity
    )


def gathered_once(array, axis):
    leaves = jax.tree.leaves(array)
    turns = sorted(range(len(leaves)), key=lambda k: -leaves[k].size)
    width = (1, *leaves[turns[0]].shape)[-1]
    lines = [
        jnp.pad(leaves[k].reshape(-1), (0, -leaves[k].size % width)).reshape(-1, width)
        for k in turns
    ]
    both, at, found = (lax.all_gather(jnp.concatenate(lines), axis), 0, {})
    for k, line in zip(turns, lines):
        section = both[:, at : at + len(line)].reshape(len(both), -1)
        found[k] = section[:, : leaves[k].size].reshape(-1, *leaves[k].shape)
        at += len(line)
    numbers = iter(range(len(leaves)))
    return jax.tree.map(lambda _: found[next(numbers)], array)


def carried_in(array, axes, combine, identity):
    before = start = filled_with(array, identity)
    total = array
    for axis in reversed(axes):
        length, place = (lax.axis_size(axis), lax.axis_index(axis))
        pieces = gathered_once(
            jax.tree.map(
                lambda part, kind: part.astype(kind),
                total,
                (jnp.bfloat16, jnp.bfloat16, jnp.bfloat16, jnp.bfloat16),
            ),
            axis,
        )
        inside, total = (start, start)
        for k in range(length):
            passed = k < place
            total = combine(
                total, jax.tree.map(lambda part, own: part[k].astype(own.dtype), pieces, array)
            )
            inside = jax.tree.map(lambda new, old: jnp.where(passed, new, old), total, inside)
        before = combine(inside, before)
    return before


def from_everyone(array, axis):
    length = lax.axis_size(axis)
    return lax.all_to_all(
        jnp.broadcast_to(array[None], (length, *array.shape)), axis, 0, 0, tiled=True
    )


def taken_together(array, axis):
    return from_everyone(array, axis).sum(axis=0)


def in_one_piece(arrays, axis, dim, along):
    widths = [math.prod(a.shape[along:]) for a in arrays]
    both = jnp.concatenate(
        [a.reshape(*a.shape[:along], w) for a, w in zip(arrays, widths)], axis=along
    )
    whole = lax.all_gather(both, axis, axis=dim, tiled=True)
    blocks = jnp.split(whole, [sum(widths[:k]) for k in range(1, len(widths))], axis=along)
    return tuple(
        (b.reshape(*whole.shape[:along], *a.shape[along:]) for a, b in zip(arrays, blocks))
    )


def join_parts(earlier_part, later_part):
    early_decay, early_state, early_first, early_last = earlier_part
    late_decay, late_state, late_first, late_last = later_part
    linked = (early_last == late_first) & (late_first == late_last)
    passed = jnp.where(linked, jnp.exp(late_decay), 0.0)
    joined_state = jnp.where(
        late_first[:, None, None] < 0, early_state, late_state + passed[:, None, None] * early_state
    )
    joined_first = jnp.where(early_first < 0, late_first, early_first)
    joined_last = jnp.where(late_last < 0, early_last, late_last)
    return (early_decay + late_decay, joined_state, joined_first, joined_last)


def lightning_part(lin_query, lin_key, lin_value, lin_gate, log_decay, norm_gain, doc_ids):
    tok_rows = lin_query.shape[0]
    cumul = jnp.cumsum(log_decay, axis=0)
    block_decay = cumul[-1]
    doc_float = doc_ids.astype(jnp.float32)
    first_doc = doc_float[:1]
    last_doc = doc_float[-1:]
    token_order = jnp.arange(tok_rows)
    visible = (token_order[None, :] <= token_order[:, None]) & (
        doc_ids[None, :] == doc_ids[:, None]
    )
    cumul_heads = jnp.transpose(cumul)
    decay_gap = cumul_heads[:, :, None] - cumul_heads[:, None, :]
    factor = jnp.where(visible[None], jnp.exp(jnp.where(visible[None], decay_gap, 0.0)), 0.0)
    scores = jnp.einsum("thd,shd->hts", lin_query, lin_key, preferred_element_type=jnp.float32)
    weights = (scores * factor).astype(jnp.bfloat16)
    inner_part = jnp.einsum("hts,shd->thd", weights, lin_value, preferred_element_type=jnp.float32)
    tail_mask = (doc_ids == doc_ids[-1]).astype(jnp.float32)
    key_scale = jnp.exp(block_decay[None, :] - cumul) * tail_mask[:, None]
    scaled_keys = (lin_key * key_scale[:, :, None]).astype(jnp.bfloat16)
    own_state = jnp.einsum(
        "shd,she->hde", scaled_keys, lin_value, preferred_element_type=jnp.float32
    )
    identity_part = (
        jnp.zeros_like(block_decay),
        jnp.zeros_like(own_state),
        jnp.full((1,), -1.0, jnp.float32),
        jnp.full((1,), -1.0, jnp.float32),
    )
    prefix = carried_in(
        (block_decay, own_state, first_doc, last_doc), SEQ, join_parts, identity_part
    )
    prior_state = prefix[1]
    prior_doc = prefix[3]
    carried = jnp.einsum(
        "thd,hde->the",
        lin_query,
        prior_state.astype(jnp.bfloat16),
        preferred_element_type=jnp.float32,
    )
    open_mask = (doc_float == prior_doc).astype(jnp.float32)
    carried = carried * (jnp.exp(cumul) * open_mask[:, None])[:, :, None]
    mixed_heads = inner_part + carried
    square_sum = taken_together(jnp.sum(mixed_heads * mixed_heads, axis=(1, 2)), "tp")
    inv_rms = lax.rsqrt(square_sum / (HEADS * HEAD_DIM) + 1e-06)
    gated = jax.nn.sigmoid(lin_gate.astype(jnp.float32))
    return (mixed_heads * inv_rms[:, None, None] * norm_gain[None] * gated).astype(jnp.bfloat16)


def softmax_part(soft_query, soft_key, soft_value, doc_ids):
    tok_rows = soft_query.shape[0]
    heads_here = soft_query.shape[1]
    head_width = soft_query.shape[2]
    seq_index = lax.axis_index(SEQ)
    group_size = HEADS // KV_HEADS
    kv_here = max(1, heads_here // group_size)
    per_group = heads_here // kv_here
    kv_start = lax.axis_index("tp") * heads_here // group_size
    key_here = lax.dynamic_slice_in_dim(soft_key, kv_start, kv_here, 1)
    value_here = lax.dynamic_slice_in_dim(soft_value, kv_start, kv_here, 1)
    queries = soft_query.reshape(tok_rows, kv_here, per_group, head_width)
    query_docs = doc_ids.astype(jnp.float32)
    query_pos = seq_index * tok_rows + jnp.arange(tok_rows)
    last_pos = seq_index * tok_rows + tok_rows - 1
    score_scale = HEAD_DIM ** (-0.5)

    def attend(state, key_block, value_block, key_docs):
        top_score, total_weight, weighted = state
        count_here = key_block.shape[0]
        key_pos = jnp.arange(count_here)
        visible = (key_pos[None, :] <= query_pos[:, None]) & (
            key_docs.astype(jnp.float32)[None, :] == query_docs[:, None]
        )
        score = (
            jnp.einsum("tkgd,skd->kgts", queries, key_block, preferred_element_type=jnp.float32)
            * score_scale
        )
        score = jnp.where(visible, score, -1e30)
        new_top = jnp.maximum(top_score, jnp.max(score, axis=-1))
        soft_exp = jnp.where(visible, jnp.exp(score - new_top[..., None]), 0.0)
        total_weight = jnp.sum(soft_exp, axis=-1)
        weighted = jnp.einsum(
            "kgts,skd->kgtd",
            soft_exp.astype(jnp.bfloat16),
            value_block,
            preferred_element_type=jnp.float32,
        )
        return (new_top, total_weight, weighted)

    def skip_block(state):
        return state

    start_state = (
        jnp.full((kv_here, per_group, tok_rows), -1e30, jnp.float32),
        jnp.zeros((kv_here, per_group, tok_rows), jnp.float32),
        jnp.zeros((kv_here, per_group, tok_rows, head_width), jnp.float32),
    )
    key_docs = doc_ids.astype(jnp.bfloat16)
    key_block, value_block, block_docs = in_one_piece((key_here, value_here, key_docs), SEQ, 0, 1)
    state = lax.cond(
        jnp.int32(0) <= last_pos,
        lambda inner_state: attend(inner_state, key_block, value_block, block_docs),
        skip_block,
        start_state,
    )
    top_score, total_weight, weighted = state
    result = weighted / total_weight[..., None]
    return (
        jnp.transpose(result, (2, 0, 1, 3))
        .reshape(tok_rows, heads_here, head_width)
        .astype(jnp.bfloat16)
    )


def body(
    lin_query,
    lin_key,
    lin_value,
    lin_gate,
    log_decay,
    norm_gain,
    doc_ids,
    soft_query,
    soft_key,
    soft_value,
):
    lin_out = lightning_part(lin_query, lin_key, lin_value, lin_gate, log_decay, norm_gain, doc_ids)
    soft_out = softmax_part(soft_query, soft_key, soft_value, doc_ids)
    return (lin_out, soft_out)


def solution(mesh):
    split = Mesh(mesh.devices.reshape(8, 4, mesh.shape["tp"]), ("seq_0", "seq_1", "tp"))
    placed = (
        P(SEQ, "tp", None),
        P(SEQ, "tp", None),
        P(SEQ, "tp", None),
        P(SEQ, "tp", None),
        P(SEQ, "tp"),
        P("tp", None),
        P(SEQ),
        P(SEQ, "tp", None),
        P(SEQ, None, None),
        P(SEQ, None, None),
    )
    return jax.shard_map(
        body,
        mesh=split,
        in_specs=placed,
        out_specs=(P(SEQ, "tp", None), P(SEQ, "tp", None)),
        check_vma=False,
    )
```

profile of v0, /device:TPU:6, one launch (start us, length us, event | category | flops | bytes accessed | tf_op | source)
XLA Modules:
  0.0 223.7 jit_solution(17648509944787442675)
XLA Ops:
  7.3 0.8 fusion.73
  8.1 1.5 constant_dynamic-slice_fusion
  9.8 0.7 pad_maximum_fusion
  10.5 1.3 slice.254
  11.8 0.7 reshape.524
  12.5 0.6 reduce-window.6
  13.1 0.2 slice_reduce_fusion
  13.2 0.2 reduce-window.9
  13.5 0.2 slice_reduce_fusion.1
  13.7 1.3 compare_convert_fusion.1
  15.1 0.1 copy.228
  15.2 0.6 slice.256
  15.8 0.6 pad_bitcast_fusion.3
  16.5 0.7 select_bitcast_fusion
  17.1 1.2 multiply_convert_fusion.1
  18.4 0.2 convolution_convert_fusion
  18.6 19.2 %all-gather.2 = bf16[4,259,128]{2,1,0:T(8,128)(2,1)S(1)} all-gather(bf16[1,259,128]{2,1,0:T(8,128)(2,1)S(1)} %maximum_bitcast_fusion), channel_id=2, replica_groups=mesh['seq_0'=8,'seq_1'=4,'tp'=32] {'seq_1'}, dimensions={0}, use_global_device_ids=true | all-gather | bytes 331520 | tf_op jit(solution)/shard_map/all_gather | solution.py:29
  37.8 0.5 fusion.75
  39.0 0.6 fusion.74
  57.4 0.2 fusion.37
  57.6 29.3 %all-gather.3 = bf16[8,259,128]{2,1,0:T(8,128)(2,1)S(1)} all-gather(bf16[1,259,128]{2,1,0:T(8,128)(2,1)S(1)} %maximum_bitcast_fusion.1), channel_id=3, replica_groups=mesh['seq_0'=8,'seq_1'=4,'tp'=32] {'seq_0'}, dimensions={0}, use_global_device_ids=true | all-gather | bytes 596736 | tf_op jit(solution)/shard_map/all_gather | solution.py:29
  86.9 0.6 fusion.72
  88.2 0.6 fusion.71
  118.8 0.1 copy.234
  118.9 0.1 copy.235
  119.0 0.1 copy.236
  119.2 0.1 copy.237
  119.3 0.1 copy.238
  119.4 0.1 copy.239
  119.5 0.1 copy.240
  119.6 0.1 copy.241
  120.5 0.5 fusion.26
  121.0 0.5 multiply_reduce_fusion
  121.4 0.6 broadcast_in_dim.378
  122.1 18.6 %all-to-all-start = ((f32[32,1,256]{2,1,0:T(1,128)}), f32[32,1,256]{2,1,0:T(1,128)S(1)}, u32[]{:S(2)}, u32[]{:S(2)}) async-start(f32[32,1,256]{2,1,0:T(1,128)} %broadcast_in_dim.378), calls=%async_computation | async-start | bytes 65536 | tf_op jit(solution)/shard_map/all_to_all | solution.py:64
  140.7 0.1 copy.248
  140.8 9.5 %all-to-all-done = f32[32,1,256]{2,1,0:T(1,128)S(1)} async-done(((f32[32,1,256]{2,1,0:T(1,128)}), f32[32,1,256]{2,1,0:T(1,128)S(1)}, u32[]{:S(2)}, u32[]{:S(2)}) %all-to-all-start) | async-done | bytes 32800 | tf_op jit(solution)/shard_map/all_to_all | solution.py:64
  150.4 0.1 multiply_convert_fusion
  150.5 0.8 copy.253
  151.3 43.2 %all-gather.6.cloned.1.call-done = bf16[8192,257]{1,0:T(8,128)(2,1)} async-done(((bf16[256,257]{1,0:T(8,128)(2,1)}), bf16[8192,257]{1,0:T(8,128)(2,1)}) %all-gather.6.cloned.1.call-update) | async-done | bytes 4210704 | tf_op jit(solution)/shard_map/all_gather | solution.py:78
  194.5 21.4 %conditional.1 = (f32[1,2,256]{2,1,0:T(2,128)S(1)}, f32[1,2,256,128]{3,2,1,0:T(8,128)S(1)}) conditional(s32[]{:T(128)} %convert_element_type.536, () %tuple.16, (s32[]{:T(128)}, s32[256]{0:T(256)S(1)}, bf16[8192,257]{1,0:T(8,128)(2,1)}, f32[256]{0:T(256)S(1)}, bf16[256,2,128]{2,1,0:T(2,128)(2,1)S(1)}) %tuple.93), branch_computations={%region_4.5_spmd, %region_5.8_spmd} | conditional | flops 2208308992 | bytes 63406100 | solution.py:197
  194.5 2.2 convert_reduce_fusion
  196.8 3.5 %fusion.6 = pred[256,8192]{0,1:T(8,128)(4,1)S(1)} fusion(f32[256]{0:T(256)S(1)} %get-tuple-element.24, s32[256]{0:T(256)S(1)} %broadcast_add_fusion, f32[8192]{0:T(1024)S(1)} %convert_reduce_fusion), kind=kLoop, calls=%fused_computation.8 | loop fusion | flops 6291456 | bytes 2131968 | tf_op jit(solution)/shard_map/cond/branch_1_fun/and | solution.py:168
  200.3 4.4 %fusion = (f32[2,256]{1,0:T(2,128)S(1)}, f32[8192,256,2]{1,0,2:T(8,128)S(1)}) fusion(pred[256,8192]{0,1:T(8,128)(4,1)S(1)} %fusion.6, bf16[256,2,128]{2,1,0:T(2,128)(2,1)S(1)} %get-tuple-element.87, bf16[8192,257]{1,0:T(8,128)(2,1)} %get-tuple-element.23), kind=kOutput, calls=%fused_computation.2 | convolution fusion | flops 1086324224 | bytes 21104640 | tf_op jit(solution)/shard_map/cond/branch_1_fun/tkgd,skd->kgts/dot_general | solution.py:172
  204.7 6.8 %fusion.13 = f32[1,2,256,128]{3,2,1,0:T(8,128)S(1)} fusion(bf16[8192,257]{1,0:T(8,128)(2,1)} %get-tuple-element.23, f32[8192,256,2]{1,0,2:T(8,128)S(1)} %get-tuple-element.93, f32[2,256]{1,0:T(2,128)S(1)} %broadcast_maximum_fusion, pred[256,8192]{0,1:T(8,128)(4,1)S(1)} %fusion.6), kind=kOutput, calls=%fused_computation.16 | convolution fusion | flops 1094713344 | bytes 21235712 | tf_op jit(solution)/shard_map/cond/branch_1_fun/kgts,skd->kgtd/dot_general | solution.py:179
  211.5 4.5 %fusion.2 = f32[2,256]{1,0:T(2,128)S(1)} fusion(f32[8192,256,2]{1,0,2:T(8,128)S(1)} %get-tuple-element.93, f32[2,256]{1,0:T(2,128)S(1)} %broadcast_maximum_fusion, pred[256,8192]{0,1:T(8,128)(4,1)S(1)} %fusion.6), kind=kLoop, calls=%fused_computation.4 | loop fusion | flops 20971008 | bytes 18878464 | tf_op jit(solution)/shard_map/cond/branch_1_fun/reduce_sum | solution.py:178
  215.9 0.1 fusion.44
  216.1 0.8 copy.254
  (57 shorter events, 1.4 us)
Async XLA Ops:
  7.2 11.2 %copy-start = (bf16[256,2,128]{2,1,0:T(2,128)(2,1)S(1)}, bf16[256,2,128]{2,1,0:T(2,128)(2,1)}, u32[]{:S(2)}) copy-start(bf16[256,2,128]{2,1,0:T(2,128)(2,1)} %param.14) | copy-start | bytes 393220
  7.2 113.1 %copy-start.3 = (s32[256]{0:T(256)S(1)}, s32[256]{0:T(256)}, u32[]{:S(2)}) copy-start(s32[256]{0:T(256)} %param.18) | copy-start | bytes 3076
  7.2 113.8 %copy-start.1 = (bf16[256,2,128]{2,1,0:T(2,128)(2,1)S(1)}, bf16[256,2,128]{2,1,0:T(2,128)(2,1)}, u32[]{:S(2)}) copy-start(bf16[256,2,128]{2,1,0:T(2,128)(2,1)} %param.13) | copy-start | bytes 393220
  7.2 113.3 %copy-start.5 = (bf16[256,2,128]{2,1,0:T(2,128)(2,1)S(1)}, bf16[256,2,128]{2,1,0:T(2,128)(2,1)}, u32[]{:S(2)}) copy-start(bf16[256,2,128]{2,1,0:T(2,128)(2,1)} %param.12) | copy-start | bytes 393220
  7.2 133.5 %copy-start.2 = (bf16[256,2,128]{2,1,0:T(2,128)(2,1)S(1)}, bf16[256,2,128]{2,1,0:T(2,128)(2,1)}, u32[]{:S(2)}) copy-start(bf16[256,2,128]{2,1,0:T(2,128)(2,1)} %param.15) | copy-start | bytes 393220
  7.2 143.1 %copy-start.4 = (f32[2,128]{1,0:T(2,128)S(1)}, f32[2,128]{1,0:T(2,128)}, u32[]{:S(2)}) copy-start(f32[2,128]{1,0:T(2,128)} %param.17) | copy-start | bytes 3076
  7.2 187.3 %copy-start.6 = (bf16[256,2,128]{2,1,0:T(2,128)(2,1)S(1)}, bf16[256,2,128]{2,1,0:T(2,128)(2,1)}, u32[]{:S(2)}) copy-start(bf16[256,2,128]{2,1,0:T(2,128)(2,1)} %param.19) | copy-start | bytes 393220
  7.2 187.3 %all-gather.6.cloned.1.call-start = ((), (), s32[]{:S(2)}) async-start(), calls=%async_computation.1 | async-start | bytes 6488064 | tf_op jit(solution)/shard_map/all_gather | solution.py:78
  122.1 28.2 %all-to-all-start = ((f32[32,1,256]{2,1,0:T(1,128)}), f32[32,1,256]{2,1,0:T(1,128)S(1)}, u32[]{:S(2)}, u32[]{:S(2)}) async-start(f32[32,1,256]{2,1,0:T(1,128)} %broadcast_in_dim.378), calls=%async_computation | async-start | bytes 65536 | tf_op jit(solution)/shard_map/all_to_all | solution.py:64
Sparse Core Ops, SparseCore 0:
  10.7 183.7 all-gather.5
where the time goes:
time: 225 us; the launch traced here: 224 us
  between operations  63.2 us (28%)
  waiting for transfers between devices  52.7 us (23%)
  blocking collectives  48.5 us (22%)
  starting transfers between devices  18.6 us (8%)
  other arithmetic  16.7 us (7%)
  matrix products  12.4 us (6%)
  local copies, waits for them, and re-layouts  11.6 us (5%)
    all_gather x2, blocking collectives, gathered_once(): both, at, found = (lax.all_gather(jnp.concatenate(lines), axis), 0, {})  48.5 us
    all_gather x1, waiting for transfers between devices, in_one_piece(): whole = lax.all_gather(both, axis, axis=dim, tiled=True)  43.2 us
    all_to_all x1, starting transfers between devices, from_everyone(): lax.all_to_all(jnp.broadcast_to(array[None], (length, *array.shape)), axi...  18.6 us
    all_to_all x1, waiting for transfers between devices, from_everyone(): lax.all_to_all(jnp.broadcast_to(array[None], (length, *array.shape)), axi...  9.49 us
    dot_general x1, matrix products, attend(): jnp.einsum('kgts,skd->kgtd', soft_exp.astype(jnp.bfloat16), value_block,...  6.76 us
  transfers between devices with their start and end apart: 2, of which 2 were waited for; matrix products, arithmetic and copies ran while one was open for 7% of the time, Pallas kernels for 0%

commit v1 on v0

v1 whole, which is shorter than its diff:
```python
import functools

import jax
import jax.numpy as jnp
from jax import lax
from jax.experimental import pallas as pl
from jax.experimental.pallas import tpu as pltpu
from jax.sharding import Mesh
from jax.sharding import PartitionSpec as P

HEADS = 64
HEAD_DIM = 128
KV_HEADS = 8
SEQ = ("y", "z")
TP = ("w", "x", "c")
MESH = pl.DeviceIdType.MESH
F32 = jnp.float32
BF16 = jnp.bfloat16
BACK = 5
LOW = -1e30


def dot_nt(a, b, **kw):
    return lax.dot_general(a, b, (((1,), (1,)), ((), ())), preferred_element_type=F32, **kw)


def dot_tn(a, b):
    return lax.dot_general(a, b, (((0,), (0,)), ((), ())), preferred_element_type=F32)


def dot_nn(a, b):
    return lax.dot_general(a, b, (((1,), (0,)), ((), ())), preferred_element_type=F32)


def as_column(row, toks):
    return jnp.concatenate(
        [
            jnp.transpose(jnp.broadcast_to(row[:, k : k + 128], (128, 128)))
            for k in range(0, toks, 128)
        ],
        axis=0,
    )


def three_parts(line):
    high = line.astype(BF16)
    rest = line - high.astype(F32)
    middle = rest.astype(BF16)
    low = (rest - middle.astype(F32)).astype(BF16)
    row = lax.broadcasted_iota(jnp.int32, (16, 128), 0)
    parts = [jnp.broadcast_to(p.astype(F32), (16, 128)) for p in (high, middle, low)]
    return jnp.where(
        row == 0, parts[0], jnp.where(row == 1, parts[1], jnp.where(row == 2, parts[2], 0.0))
    ).astype(BF16)


def from_parts(tile):
    wide = tile.astype(F32)
    return wide[0:1] + wide[1:2] + wide[2:3]


def kernel(
    sizes,
    lq,
    lk,
    lv,
    lg,
    ld,
    gain,
    docs,
    sq,
    sk,
    sv,
    lin_out,
    soft_out,
    kv,
    wide8,
    wq,
    wk,
    wv,
    wg,
    wo,
    dec,
    ccol,
    dcol,
    dq,
    mix,
    s_out,
    s_in,
    t_out,
    t_in,
    p_out,
    p_in,
    run_state,
    run_decay,
    pdoc,
    ss_in,
    m_scr,
    l_scr,
    acc,
    p_sem,
    x_sem,
    c_sem,
    s_sem,
    t_sem,
    st_sem,
    ss_sem,
    za_snd,
    a_snd,
    a5_snd,
    b_snd,
    x_snd,
    s_snd,
    t_snd,
    p_snd,
    ss_snd,
):
    n_y, n_z, n_w, n_x, n_c = sizes
    n_tp = n_w * n_x * n_c
    toks = lq.shape[0] // 2
    y, z, w = (lax.axis_index("y"), lax.axis_index("z"), lax.axis_index("w"))
    x, c = (lax.axis_index("x"), lax.axis_index("c"))
    tp = (w * n_x + x) * n_c + c
    half = lax.rem(x, 2)
    other_half = 1 - half
    x_mate = x + 1 - 2 * half
    c_mate = 1 - c
    head = (tp * 2) // (HEADS // KV_HEADS)

    def tp_place(k):
        t2 = lax.rem(tp + k, n_tp)
        return {"w": t2 // (n_x * n_c), "x": lax.rem(t2 // n_c, n_x), "c": lax.rem(t2, n_c)}

    barrier = pltpu.get_barrier_semaphore()

    def greet_tp(k, carry):
        pl.semaphore_signal(barrier, inc=1, device_id=tp_place(k), device_id_type=MESH)
        return carry

    def greet_y(k, carry):
        pl.semaphore_signal(
            barrier, inc=1, device_id={"y": lax.rem(y + k, n_y)}, device_id_type=MESH
        )
        return carry

    for k in range(1, n_z):
        pl.semaphore_signal(
            barrier, inc=1, device_id={"z": lax.rem(z + k, n_z)}, device_id_type=MESH
        )
    lax.fori_loop(1, n_y, greet_y, 0)
    lax.fori_loop(1, n_tp, greet_tp, 0)

    def send(src, dst, send_sem, recv_sem, device):
        pltpu.make_async_remote_copy(
            src_ref=src,
            dst_ref=dst,
            send_sem=send_sem,
            recv_sem=recv_sem,
            device_id=device,
            device_id_type=MESH,
        ).start()

    def landed(ref, sem):
        pltpu.make_async_remote_copy(
            src_ref=ref,
            dst_ref=ref,
            send_sem=a5_snd.at[0],
            recv_sem=sem,
            device_id={"c": c_mate},
            device_id_type=MESH,
        ).wait_recv()

    def left(ref, sem):
        pltpu.make_async_remote_copy(
            src_ref=ref,
            dst_ref=ref,
            send_sem=sem,
            recv_sem=p_sem.at[0],
            device_id={"c": c_mate},
            device_id_type=MESH,
        ).wait_send()

    doc_row = docs[...].astype(F32)
    pack_row = lax.broadcasted_iota(jnp.int32, (16, 128), 0)
    doc_tile = jnp.zeros((16, 128), F32)
    for k in range(toks // 128):
        piece = jnp.broadcast_to(doc_row[:, 128 * k : 128 * (k + 1)], (16, 128))
        doc_tile = jnp.where(pack_row == k, piece, doc_tile)
    doc_tile = doc_tile.astype(BF16)
    for kind, source in ((0, sk), (1, sv)):
        wide8[kind] = source[...].astype(F32)
        kv[kind, z, 0:toks, :] = wide8[kind, pl.ds(head, toks, stride=KV_HEADS), :].astype(BF16)
        kv[kind, z, toks : toks + 16, :] = doc_tile

    doc_col = as_column(doc_row, toks)
    dcol[...] = doc_col
    for h in range(2):
        dq[pl.ds(h, toks, stride=2), :] = doc_col
    for source, target in ((lq, wq), (lk, wk), (lv, wv), (lg, wg)):
        target[...] = source[...].astype(F32)

    dec[...] = jnp.zeros_like(dec)
    dec[0:2, :] = ld[...]
    t_id = lax.broadcasted_iota(jnp.int32, (toks, toks), 0)
    s_id = lax.broadcasted_iota(jnp.int32, (toks, toks), 1)
    upto = (s_id <= t_id).astype(F32)
    cum_col = dot_nt(upto, dec[...], precision=lax.Precision.HIGHEST)
    cum_row = dot_nt(dec[...], upto, precision=lax.Precision.HIGHEST)
    ccol[...] = cum_col
    last_doc = doc_row[:, toks - 1 : toks]
    tail = (doc_col[:, :1] == last_doc).astype(F32)
    queries = [wq[pl.ds(h, toks, stride=2), :].astype(BF16) for h in range(2)]
    keys = [wk[pl.ds(h, toks, stride=2), :] for h in range(2)]
    values = [wv[pl.ds(h, toks, stride=2), :].astype(BF16) for h in range(2)]
    decay_line = jnp.zeros((1, 128), F32)
    lane = lax.broadcasted_iota(jnp.int32, (1, 128), 1)
    for h in range(2):
        end = cum_col[toks - 1 : toks, h : h + 1]
        scale = jnp.exp(end - cum_col[:, h : h + 1]) * tail
        state = dot_tn((keys[h] * scale).astype(BF16), values[h]).astype(BF16)
        for q in range(4):
            s_out[q, 32 * h : 32 * h + 32, :] = state[32 * q : 32 * q + 32, :]
        decay_line = jnp.where(lane == h, end, decay_line)
    decay_line = jnp.where(lane == 2, last_doc, decay_line)
    scalars = three_parts(decay_line)
    for q in range(4):
        s_out[q, 64:80, :] = scalars
    s_in[z] = s_out[z]
    visible = (s_id <= t_id) & (doc_row == doc_col[:, :1])
    for h in range(2):
        gap = cum_col[:, h : h + 1] - cum_row[h : h + 1, :]
        factor = jnp.where(visible, jnp.exp(jnp.where(visible, gap, 0.0)), 0.0)
        weights = (dot_nt(queries[h], keys[h].astype(BF16)) * factor).astype(BF16)
        mix[h] = dot_nn(weights, values[h])
    m_scr[...] = jnp.full_like(m_scr, LOW)
    l_scr[...] = jnp.zeros_like(l_scr)
    acc[...] = jnp.zeros_like(acc)

    pl.semaphore_wait(barrier, (n_z - 1) + (n_y - 1) + (n_tp - 1))

    for k in range(1, n_z):
        z2 = lax.rem(z + k, n_z)
        send(s_out.at[z2], s_in.at[z], s_snd.at[k - 1], s_sem.at[z], {"z": z2})
    owner = ((z == 0) | (z == 3)) == (half == 0)

    @pl.when(owner)
    def _():
        for k in range(1, n_z):
            z2 = lax.rem(z + k, n_z)
            send(kv.at[c, z], kv.at[c, z], za_snd.at[k - 1], p_sem.at[z // 2], {"z": z2})

    for k in range(1, n_z):
        z2 = lax.rem(z + k, n_z)
        landed(s_in.at[z2], s_sem.at[z2])
    lines = [from_parts(s_in[k, 64:80, :]) for k in range(4)]
    ends = [line[:, 2:3] for line in lines]

    def weight_of(first, last, h, doc):
        total = jnp.zeros((1, 1), F32)
        for k in range(first, last + 1):
            total = total + lines[k][:, h : h + 1]
        return jnp.where(doc == ends[last], jnp.exp(total), 0.0)

    total_line = lines[0] + lines[1] + lines[2] + lines[3]
    for h in range(2):
        rows = slice(32 * h, 32 * h + 32)
        total = s_in[3, rows, :].astype(F32)
        for k in range(3):
            total = total + s_in[k, rows, :].astype(F32) * weight_of(k + 1, 3, h, ends[k])
        t_out[rows, :] = total.astype(BF16)
    t_out[64:80, :] = three_parts(jnp.where(lane == 2, ends[3], total_line))
    for d in range(1, BACK + 1):

        @pl.when(y + d < n_y)
        def _(d=d):
            send(t_out, t_in.at[d], t_snd.at[d], t_sem.at[d], {"y": y + d})

    def place(which, j):
        return which + j * (3 - 2 * which)

    def primary(d):
        for j in range(2):
            zz = place(half, j)
            unit = kv.at[c, 4 * d + zz]
            mine = (d == 0) & (zz == z)

            @pl.when(jnp.logical_not(mine))
            def _():
                landed(unit, p_sem.at[2 * d + j])

            @pl.when((y + 1 < n_y) & (d + 1 < BACK))
            def _():
                send(
                    unit,
                    kv.at[c, 4 * d + 4 + zz],
                    a_snd.at[2 * d + j],
                    p_sem.at[2 * d + 2 + j],
                    {"y": lax.rem(y + 1, n_y)},
                )

            @pl.when((y + BACK < n_y) & (d == 0))
            def _():
                send(
                    unit,
                    kv.at[c, 4 * BACK + zz],
                    a5_snd.at[j],
                    p_sem.at[2 * BACK + j],
                    {"y": lax.rem(y + BACK, n_y)},
                )

            @pl.when(jnp.logical_not(mine))
            def _():
                send(unit, unit, x_snd.at[2 * d + j], x_sem.at[2 * d + j], {"x": x_mate})
                send(unit, unit, b_snd.at[4 * d + zz], c_sem.at[4 * d + zz], {"c": c_mate})

    def secondary(d):
        for j in range(2):
            zz = place(other_half, j)
            unit = kv.at[c, 4 * d + zz]

            @pl.when(jnp.logical_not((d == 0) & (zz == z)))
            def _():
                landed(unit, x_sem.at[2 * d + j])
                send(unit, unit, b_snd.at[4 * d + zz], c_sem.at[4 * d + zz], {"c": c_mate})

    def complete(d):
        for zz in range(4):

            @pl.when(jnp.logical_not((d == 0) & (zz == z)))
            def _():
                landed(kv.at[c_mate, 4 * d + zz], c_sem.at[4 * d + zz])

    score_scale = HEAD_DIM ** (-0.5)
    rows_per = 128

    def attend(d):
        def chunk(i, carry):
            first = pl.multiple_of(i * rows_per, rows_per)
            rows = pl.ds(first, rows_per)
            query = sq[rows, :]
            query_doc = dq[rows, :][:, :1]
            line_id = lax.broadcasted_iota(jnp.int32, (rows_per, toks), 0) + first
            query_pos = lax.shift_right_logical(line_id, 1) + z * toks
            key_id = lax.broadcasted_iota(jnp.int32, (rows_per, toks), 1)
            scores = []
            for zz in range(4):
                slot = 4 * d + zz
                tile = kv[0, slot, toks : toks + 16, :].astype(F32)
                key_doc = jnp.concatenate([tile[k : k + 1] for k in range(toks // 128)], axis=1)
                seen = (key_doc == query_doc) & (key_id + (zz - 4 * d) * toks <= query_pos)
                score = dot_nt(query, kv[0, slot, 0:toks, :])
                scores.append(jnp.where(seen, score, LOW))
            top = functools.reduce(jnp.maximum, scores)
            old_top = m_scr[rows, :][:, :1]
            new_top = jnp.maximum(old_top, jnp.max(top, axis=1, keepdims=True))
            shrink = jnp.exp((old_top - new_top) * score_scale)
            exps = [jnp.exp((score - new_top) * score_scale) for score in scores]
            added = jnp.sum(functools.reduce(jnp.add, exps), axis=1, keepdims=True)
            weighted = jnp.zeros((rows_per, HEAD_DIM), F32)
            for zz in range(4):
                weighted = weighted + dot_nn(exps[zz].astype(BF16), kv[1, 4 * d + zz, 0:toks, :])
            m_scr[rows, :] = jnp.broadcast_to(new_top, (rows_per, 128))
            l_scr[rows, :] = l_scr[rows, :] * shrink + added
            acc[rows, :] = acc[rows, :] * shrink + weighted
            return carry

        lax.fori_loop(0, 2 * toks // rows_per, chunk, 0)

    def row_prefixes():
        run_state[...] = jnp.zeros_like(run_state)
        run_decay[...] = jnp.zeros_like(run_decay)
        pdoc[...] = jnp.full_like(pdoc, -1.0)
        for d in range(1, BACK + 1):

            @pl.when(y >= d)
            def _(d=d):
                landed(t_in.at[d], t_sem.at[d])
                line = from_parts(t_in[d, 64:80, :])
                end = line[:, 2:3]
                if d == 1:
                    pdoc[...] = jnp.broadcast_to(end, pdoc.shape)
                for h in range(2):
                    rows = slice(32 * h, 32 * h + 32)
                    passed = run_decay[0:1, h : h + 1]
                    keep = jnp.where(end == pdoc[0:1, 0:1], jnp.exp(passed), 0.0)
                    run_state[rows, :] = run_state[rows, :] + t_in[d, rows, :].astype(F32) * keep
                run_decay[...] = run_decay[...] + line

        before = pdoc[0:1, 0:1]
        for h in range(2):
            rows = slice(32 * h, 32 * h + 32)
            entry = run_state[rows, :]
            p_out[0, rows, :] = entry.astype(BF16)
            for k in range(1, 4):
                prior = entry * weight_of(0, k - 1, h, before)
                for j in range(k):
                    part = s_in[j, rows, :].astype(F32)
                    if j < k - 1:
                        part = part * weight_of(j + 1, k - 1, h, ends[j])
                    prior = prior + part
                p_out[k, rows, :] = prior.astype(BF16)
        own_doc = before
        for k in range(1, 4):
            own_doc = jnp.where(z == k, ends[k - 1], own_doc)
        pdoc[...] = jnp.broadcast_to(own_doc, pdoc.shape)
        p_in[z] = p_out[z]
        for k in range(1, n_z):
            z2 = lax.rem(z + k, n_z)
            send(p_out.at[z2], p_in.at[z], p_snd.at[k - 1], st_sem.at[z], {"z": z2})

    def carry_over():
        for k in range(1, n_z):
            z2 = lax.rem(z + k, n_z)
            landed(p_in.at[z2], st_sem.at[z2])
        opened = (dcol[...][:, :1] == pdoc[0:1, 0:1]).astype(F32)
        squares = jnp.zeros((toks, 128), F32)
        for h in range(2):
            rows = slice(32 * h, 32 * h + 32)
            state = jnp.concatenate([p_in[q, rows, :] for q in range(4)], axis=0)
            query = wq[pl.ds(h, toks, stride=2), :].astype(BF16)
            factor = jnp.exp(ccol[...][:, h : h + 1]) * opened
            mixed = mix[h] + dot_nn(query, state) * factor
            mix[h] = mixed
            squares = squares + mixed * mixed
        sums = dot_nt(jnp.ones((8, 128), F32), squares, precision=lax.Precision.HIGHEST)
        ss_in[tp] = sums[0:1, :]

        def post(k, carry):
            send(ss_in.at[tp], ss_in.at[tp], ss_snd.at[k], ss_sem.at[tp], tp_place(k))
            return carry

        lax.fori_loop(1, n_tp, post, 0)

    def finish_lin():
        def arrive(k, carry):
            t2 = lax.rem(tp + k, n_tp)
            landed(ss_in.at[t2], ss_sem.at[t2])
            return carry

        lax.fori_loop(1, n_tp, arrive, 0)
        total = jnp.sum(ss_in[...], axis=0)
        inv = lax.rsqrt(total / (n_tp * 2 * HEAD_DIM) + 1e-06)
        inv_col = as_column(inv, toks)
        for h in range(2):
            gate = wg[pl.ds(h, toks, stride=2), :]
            wo[pl.ds(h, toks, stride=2), :] = (
                mix[h] * inv_col * gain[h : h + 1, :] * jax.nn.sigmoid(gate)
            )
        lin_out[...] = wo[...].astype(BF16)

    def order(it):
        return jnp.where(it == 4, 5, jnp.where(it == 5, 4, it))

    primary(0)

    def step(it, carry):
        d = order(it)
        after = order(it + 1)

        @pl.when(d <= y)
        def _():
            secondary(d)

        @pl.when((it < BACK) & (after <= y))
        def _():
            primary(after)

        @pl.when(d <= y)
        def _():
            complete(d)
            attend(d)

        @pl.when(it == 0)
        def _():
            row_prefixes()

        @pl.when(it == 1)
        def _():
            carry_over()

        return carry

    lax.fori_loop(0, BACK + 1, step, 0)
    soft_out[...] = (acc[...] / l_scr[...]).astype(BF16)
    finish_lin()

    for k in range(n_z - 1):
        left(s_out.at[0], s_snd.at[k])
        left(p_out.at[0], p_snd.at[k])

        @pl.when(owner)
        def _():
            left(kv.at[c, z], za_snd.at[k])

    for d in range(1, BACK + 1):

        @pl.when(y + d < n_y)
        def _(d=d):
            left(t_out, t_snd.at[d])

    def sent(k, carry):
        left(ss_in.at[tp], ss_snd.at[k])
        return carry

    lax.fori_loop(1, n_tp, sent, 0)

    def row_sent(d, carry):
        @pl.when(d <= y)
        def _():
            for j in range(2):
                mine = (d == 0) & (place(half, j) == z)

                @pl.when((y + 1 < n_y) & (d + 1 < BACK))
                def _():
                    left(kv.at[c, 0], a_snd.at[2 * d + j])

                @pl.when((y + BACK < n_y) & (d == 0))
                def _():
                    left(kv.at[c, 0], a5_snd.at[j])

                @pl.when(jnp.logical_not(mine))
                def _():
                    left(kv.at[c, 0], x_snd.at[2 * d + j])

            for zz in range(4):

                @pl.when(jnp.logical_not((d == 0) & (zz == z)))
                def _():
                    left(kv.at[c, 0], b_snd.at[4 * d + zz])

        return carry

    lax.fori_loop(0, BACK + 1, row_sent, 0)


def body(sizes, lin_query, lin_key, lin_value, lin_gate, log_decay, norm_gain, doc_ids,
         soft_query, soft_key, soft_value):
    toks = lin_query.shape[0]
    n_tp = sizes[2] * sizes[3] * sizes[4]
    flat = lambda a: a.reshape(-1, HEAD_DIM)
    dma = pltpu.SemaphoreType.DMA
    rows = BACK + 1
    unit = toks + 16
    in_vmem = pl.BlockSpec(memory_space=pltpu.VMEM)
    lin_out, soft_out = pl.pallas_call(
        functools.partial(kernel, sizes),
        out_shape=(
            jax.ShapeDtypeStruct((2 * toks, HEAD_DIM), BF16),
            jax.ShapeDtypeStruct((2 * toks, HEAD_DIM), BF16),
        ),
        in_specs=[in_vmem] * 10,
        out_specs=(in_vmem, in_vmem),
        scratch_shapes=[
            pltpu.VMEM((2, 4 * rows, unit, 128), BF16),
            pltpu.VMEM((2, KV_HEADS * toks, 128), F32),
            pltpu.VMEM((2 * toks, 128), F32),
            pltpu.VMEM((2 * toks, 128), F32),
            pltpu.VMEM((2 * toks, 128), F32),
            pltpu.VMEM((2 * toks, 128), F32),
            pltpu.VMEM((2 * toks, 128), F32),
            pltpu.VMEM((8, toks), F32),
            pltpu.VMEM((toks, 8), F32),
            pltpu.VMEM((toks, 128), F32),
            pltpu.VMEM((2 * toks, 128), F32),
            pltpu.VMEM((2, toks, 128), F32),
            pltpu.VMEM((4, 80, 128), BF16),
            pltpu.VMEM((4, 80, 128), BF16),
            pltpu.VMEM((80, 128), BF16),
            pltpu.VMEM((rows, 80, 128), BF16),
            pltpu.VMEM((4, 64, 128), BF16),
            pltpu.VMEM((4, 64, 128), BF16),
            pltpu.VMEM((64, 128), F32),
            pltpu.VMEM((1, 128), F32),
            pltpu.VMEM((1, 128), F32),
            pltpu.VMEM((n_tp, 1, toks), F32),
            pltpu.VMEM((2 * toks, 128), F32),
            pltpu.VMEM((2 * toks, 128), F32),
            pltpu.VMEM((2 * toks, 128), F32),
            dma((2 * rows,)),
            dma((2 * rows,)),
            dma((4 * rows,)),
            dma((4,)),
            dma((rows,)),
            dma((4,)),
            dma((n_tp,)),
            dma((3,)),
            dma((2 * rows,)),
            dma((2,)),
            dma((4 * rows,)),
            dma((2 * rows,)),
            dma((3,)),
            dma((rows,)),
            dma((3,)),
            dma((n_tp,)),
        ],
        compiler_params=pltpu.CompilerParams(
            collective_id=0, has_side_effects=True, vmem_limit_bytes=48 * 1024 * 1024
        ),
    )(
        flat(lin_query),
        flat(lin_key),
        flat(lin_value),
        flat(lin_gate),
        jnp.transpose(log_decay),
        norm_gain,
        doc_ids.reshape(1, toks),
        flat(soft_query),
        flat(soft_key),
        flat(soft_value),
    )
    return lin_out.reshape(toks, 2, HEAD_DIM), soft_out.reshape(toks, 2, HEAD_DIM)


def solution(mesh, sizes=(8, 4, 2, 8, 2)):
    split = Mesh(mesh.devices.reshape(sizes), ("y", "z", "w", "x", "c"))
    placed = (
        P(SEQ, TP, None),
        P(SEQ, TP, None),
        P(SEQ, TP, None),
        P(SEQ, TP, None),
        P(SEQ, TP),
        P(TP, None),
        P(SEQ),
        P(SEQ, TP, None),
        P(SEQ, None, None),
        P(SEQ, None, None),
    )
    return jax.shard_map(
        functools.partial(body, sizes),
        mesh=split,
        in_specs=placed,
        out_specs=(P(SEQ, TP, None), P(SEQ, TP, None)),
        check_vma=False,
    )
```

time: 225 us -> 73.6 us (0.33)
  the two profiles are of different devices: /device:TPU:6 before, /device:TPU:113 now
where the time goes in v1:
time: 73.6 us; the launch traced here: 73.3 us
  Pallas kernels  64 us (87%)
  local copies, waits for them, and re-layouts  8.6 us (12%)
    pallas_call x1, Pallas kernels, body(): pl.pallas_call(functools.partial(kernel, sizes), out_shape=(jax.ShapeDtyp...  64 us
    unnamed x22, local copies, waits for them, and re-layouts  8.6 us

profile of v1, /device:TPU:113, one launch (start us, length us, event | category | flops | bytes accessed | tf_op | source)
XLA Modules:
  0.0 73.3 jit_solution(11193998655377286282)
XLA Ops:
  0.6 0.0 copy-start.9
  0.6 0.0 copy-start.7
  0.7 0.0 copy-start.8
  0.7 0.7 copy-done.9
  1.3 0.0 copy-done.7
  1.3 0.0 copy-done.8
  1.3 0.0 copy-start
  1.3 1.0 %copy-done = bf16[256,8,128]{2,1,0:T(8,128)(2,1)S(1)} copy-done((bf16[256,8,128]{2,1,0:T(8,128)(2,1)S(1)}, bf16[256,8,128]{2,1,0:T(8,128)(2,1)}, u32[]{:S(2)}) %copy-start) | copy-done | bytes 524312
  2.4 0.0 copy-start.1
  2.4 1.0 %copy-done.1 = bf16[256,8,128]{2,1,0:T(8,128)(2,1)S(1)} copy-done((bf16[256,8,128]{2,1,0:T(8,128)(2,1)S(1)}, bf16[256,8,128]{2,1,0:T(8,128)(2,1)}, u32[]{:S(2)}) %copy-start.1) | copy-done | bytes 524312
  3.4 0.0 copy-start.2
  3.4 0.9 %copy-done.2 = bf16[256,2,128]{2,1,0:T(2,128)(2,1)S(1)} copy-done((bf16[256,2,128]{2,1,0:T(2,128)(2,1)S(1)}, bf16[256,2,128]{2,1,0:T(2,128)(2,1)}, u32[]{:S(2)}) %copy-start.2) | copy-done | bytes 131096
  4.3 0.0 copy-start.3
  4.3 0.9 %copy-done.3 = bf16[256,2,128]{2,1,0:T(2,128)(2,1)S(1)} copy-done((bf16[256,2,128]{2,1,0:T(2,128)(2,1)S(1)}, bf16[256,2,128]{2,1,0:T(2,128)(2,1)}, u32[]{:S(2)}) %copy-start.3) | copy-done | bytes 131096
  5.2 0.0 copy-start.4
  5.2 0.9 %copy-done.4 = bf16[256,2,128]{2,1,0:T(2,128)(2,1)S(1)} copy-done((bf16[256,2,128]{2,1,0:T(2,128)(2,1)S(1)}, bf16[256,2,128]{2,1,0:T(2,128)(2,1)}, u32[]{:S(2)}) %copy-start.4) | copy-done | bytes 131096
  6.1 0.0 copy-start.5
  6.1 0.9 %copy-done.5 = bf16[256,2,128]{2,1,0:T(2,128)(2,1)S(1)} copy-done((bf16[256,2,128]{2,1,0:T(2,128)(2,1)S(1)}, bf16[256,2,128]{2,1,0:T(2,128)(2,1)}, u32[]{:S(2)}) %copy-start.5) | copy-done | bytes 131096
  7.0 0.0 copy-start.6
  7.1 0.9 %copy-done.6 = bf16[256,2,128]{2,1,0:T(2,128)(2,1)S(1)} copy-done((bf16[256,2,128]{2,1,0:T(2,128)(2,1)S(1)}, bf16[256,2,128]{2,1,0:T(2,128)(2,1)}, u32[]{:S(2)}) %copy-start.6) | copy-done | bytes 131096
  8.0 64.0 %shard_map.113 = (bf16[512,128]{1,0:T(8,128)(2,1)S(1)}, bf16[512,128]{1,0:T(8,128)(2,1)S(1)}) custom-call(bf16[512,128]{1,0:T(8,128)(2,1)S(1)} %bitcast.15, bf16[512,128]{1,0:T(8,128)(2,1)S(1)} %bitcast.16, bf16[512,128]{1,0:T(8,128)(2,1)S(1)} %bitcast.17, bf16[512,128]{1,0:T(8,128)(2,1)S(1)} %bitcast.18, f32[2,256]{1,0:T(2,128)S(1)} %bitcast.20, ...), custom_call_target="tpu_custom_call" | custom-call | tf_op jit(solution)/shard_map/pallas_call | solution.py:545
  72.0 0.7 copy.14
  72.6 0.7 copy.15
Async XLA Ops:
  0.6 0.7 copy-start.9
  0.6 0.7 copy-start.7
  0.7 0.7 copy-start.8
  1.3 1.0 %copy-start = (bf16[256,8,128]{2,1,0:T(8,128)(2,1)S(1)}, bf16[256,8,128]{2,1,0:T(8,128)(2,1)}, u32[]{:S(2)}) copy-start(bf16[256,8,128]{2,1,0:T(8,128)(2,1)} %param.18) | copy-start | bytes 1572868
  2.4 1.0 %copy-start.1 = (bf16[256,8,128]{2,1,0:T(8,128)(2,1)S(1)}, bf16[256,8,128]{2,1,0:T(8,128)(2,1)}, u32[]{:S(2)}) copy-start(bf16[256,8,128]{2,1,0:T(8,128)(2,1)} %param.19) | copy-start | bytes 1572868
  3.4 0.9 %copy-start.2 = (bf16[256,2,128]{2,1,0:T(2,128)(2,1)S(1)}, bf16[256,2,128]{2,1,0:T(2,128)(2,1)}, u32[]{:S(2)}) copy-start(bf16[256,2,128]{2,1,0:T(2,128)(2,1)} %param.10) | copy-start | bytes 393220
  4.3 0.9 %copy-start.3 = (bf16[256,2,128]{2,1,0:T(2,128)(2,1)S(1)}, bf16[256,2,128]{2,1,0:T(2,128)(2,1)}, u32[]{:S(2)}) copy-start(bf16[256,2,128]{2,1,0:T(2,128)(2,1)} %param.11) | copy-start | bytes 393220
  5.2 0.9 %copy-start.4 = (bf16[256,2,128]{2,1,0:T(2,128)(2,1)S(1)}, bf16[256,2,128]{2,1,0:T(2,128)(2,1)}, u32[]{:S(2)}) copy-start(bf16[256,2,128]{2,1,0:T(2,128)(2,1)} %param.12) | copy-start | bytes 393220
  6.1 0.9 %copy-start.5 = (bf16[256,2,128]{2,1,0:T(2,128)(2,1)S(1)}, bf16[256,2,128]{2,1,0:T(2,128)(2,1)}, u32[]{:S(2)}) copy-start(bf16[256,2,128]{2,1,0:T(2,128)(2,1)} %param.13) | copy-start | bytes 393220
  7.0 0.9 %copy-start.6 = (bf16[256,2,128]{2,1,0:T(2,128)(2,1)S(1)}, bf16[256,2,128]{2,1,0:T(2,128)(2,1)}, u32[]{:S(2)}) copy-start(bf16[256,2,128]{2,1,0:T(2,128)(2,1)} %param.17) | copy-start | bytes 393220

commit v2 on v1

--- a/solution.py
+++ b/solution.py
@@ -61,6 +61,18 @@
 
 def kernel(
     sizes,
+    lq_in,
+    lk_in,
+    lv_in,
+    lg_in,
+    ld_in,
+    gain_in,
+    docs_in,
+    sq_in,
+    sk_in,
+    sv_in,
+    lin_out,
+    soft_out,
     lq,
     lk,
     lv,
@@ -71,8 +83,7 @@
     sq,
     sk,
     sv,
-    lin_out,
-    soft_out,
+    in_sem,
     kv,
     wide8,
     wq,
@@ -105,6 +116,7 @@
     t_sem,
     st_sem,
     ss_sem,
+    ready,
     za_snd,
     a_snd,
     a5_snd,
@@ -117,7 +129,7 @@
 ):
     n_y, n_z, n_w, n_x, n_c = sizes
     n_tp = n_w * n_x * n_c
-    toks = lq.shape[0] // 2
+    toks = docs.shape[1]
     y, z, w = (lax.axis_index("y"), lax.axis_index("z"), lax.axis_index("w"))
     x, c = (lax.axis_index("x"), lax.axis_index("c"))
     tp = (w * n_x + x) * n_c + c
@@ -131,10 +143,31 @@
         t2 = lax.rem(tp + k, n_tp)
         return {"w": t2 // (n_x * n_c), "x": lax.rem(t2 // n_c, n_x), "c": lax.rem(t2, n_c)}
 
+    def turn(w_, x_, c_):
+        apart = jnp.minimum(x_, n_x - x_)
+        step = 2 * apart - jnp.where((x_ >= 1) & (2 * x_ <= n_x), 1, 0)
+        return (w_ * n_x + step) * n_c + c_
+
+    own_turn = turn(w, x, c)
     barrier = pltpu.get_barrier_semaphore()
 
     def greet_tp(k, carry):
-        pl.semaphore_signal(barrier, inc=1, device_id=tp_place(k), device_id_type=MESH)
+        other = tp_place(k)
+        near = ((other["x"] == x) | ((other["x"] == x_mate) & (other["c"] == c))) & (other["w"] == w)
+
+        @pl.when(near | (turn(other["w"], other["x"], other["c"]) > own_turn))
+        def _():
+            pl.semaphore_signal(barrier, inc=1, device_id=other, device_id_type=MESH)
+
+        return carry
+
+    def tell_tp(k, carry):
+        other = tp_place(k)
+
+        @pl.when(turn(other["w"], other["x"], other["c"]) < own_turn)
+        def _():
+            pl.semaphore_signal(ready, inc=1, device_id=other, device_id_type=MESH)
+
         return carry
 
     def greet_y(k, carry):
@@ -143,6 +176,25 @@
         )
         return carry
 
+    loads = [
+        pltpu.make_async_copy(source, target, in_sem.at[k])
+        for k, (source, target) in enumerate(
+            (
+                (sk_in, sk),
+                (sv_in, sv),
+                (docs_in, docs),
+                (ld_in, ld),
+                (lk_in, lk),
+                (lv_in, lv),
+                (lq_in, lq),
+                (lg_in, lg),
+                (sq_in, sq),
+                (gain_in, gain),
+            )
+        )
+    ]
+    for load in loads:
+        load.start()
     for k in range(1, n_z):
         pl.semaphore_signal(
             barrier, inc=1, device_id={"z": lax.rem(z + k, n_z)}, device_id_type=MESH
@@ -180,6 +232,8 @@
             device_id_type=MESH,
         ).wait_send()
 
+    for load in loads[:3]:
+        load.wait()
     doc_row = docs[...].astype(F32)
     pack_row = lax.broadcasted_iota(jnp.int32, (16, 128), 0)
     doc_tile = jnp.zeros((16, 128), F32)
@@ -196,6 +250,8 @@
     dcol[...] = doc_col
     for h in range(2):
         dq[pl.ds(h, toks, stride=2), :] = doc_col
+    for load in loads[3:]:
+        load.wait()
     for source, target in ((lq, wq), (lk, wk), (lv, wv), (lg, wg)):
         target[...] = source[...].astype(F32)
 
@@ -226,6 +282,33 @@
     for q in range(4):
         s_out[q, 64:80, :] = scalars
     s_in[z] = s_out[z]
+    for zz in range(4):
+        in_half = ((zz == 0) or (zz == 3)) == (half == 0)
+        for kind in range(2):
+
+            @pl.when((zz > z) & jnp.logical_not(in_half & (c == kind)))
+            def _(zz=zz, kind=kind):
+                kv[kind, zz] = jnp.full(kv.shape[2:], -1.0, BF16)
+
+            @pl.when((zz < z) & (y >= BACK))
+            def _(zz=zz, kind=kind):
+                kv[kind, 4 * BACK + zz] = jnp.full(kv.shape[2:], -1.0, BF16)
+
+    early_mates = c + jnp.where(turn(w, x_mate, c) < own_turn, 1, 0)
+    pl.semaphore_wait(barrier, (n_z - 1) + (n_y - 1) + 2 + own_turn - early_mates)
+
+    for k in range(1, n_z):
+        z2 = lax.rem(z + k, n_z)
+        send(s_out.at[z2], s_in.at[z], s_snd.at[k - 1], s_sem.at[z], {"z": z2})
+    owner = ((z == 0) | (z == 3)) == (half == 0)
+
+    @pl.when(owner)
+    def _():
+        for k in range(1, n_z):
+            z2 = lax.rem(z + jnp.where(z < 2, n_z - k, k), n_z)
+            send(kv.at[c, z], kv.at[c, z], za_snd.at[k - 1], p_sem.at[z // 2], {"z": z2})
+
+    lax.fori_loop(1, n_tp, tell_tp, 0)
     visible = (s_id <= t_id) & (doc_row == doc_col[:, :1])
     for h in range(2):
         gap = cum_col[:, h : h + 1] - cum_row[h : h + 1, :]
@@ -236,19 +319,6 @@
     l_scr[...] = jnp.zeros_like(l_scr)
     acc[...] = jnp.zeros_like(acc)
 
-    pl.semaphore_wait(barrier, (n_z - 1) + (n_y - 1) + (n_tp - 1))
-
-    for k in range(1, n_z):
-        z2 = lax.rem(z + k, n_z)
-        send(s_out.at[z2], s_in.at[z], s_snd.at[k - 1], s_sem.at[z], {"z": z2})
-    owner = ((z == 0) | (z == 3)) == (half == 0)
-
-    @pl.when(owner)
-    def _():
-        for k in range(1, n_z):
-            z2 = lax.rem(z + k, n_z)
-            send(kv.at[c, z], kv.at[c, z], za_snd.at[k - 1], p_sem.at[z // 2], {"z": z2})
-
     for k in range(1, n_z):
         z2 = lax.rem(z + k, n_z)
         landed(s_in.at[z2], s_sem.at[z2])
@@ -278,13 +348,15 @@
     def place(which, j):
         return which + j * (3 - 2 * which)
 
+    def seen_here(d, zz):
+        return jnp.logical_not(((d == 0) & (zz >= z)) | ((d == BACK) & (zz < z)))
+
     def primary(d):
         for j in range(2):
             zz = place(half, j)
             unit = kv.at[c, 4 * d + zz]
-            mine = (d == 0) & (zz == z)
-
-            @pl.when(jnp.logical_not(mine))
+
+            @pl.when(jnp.logical_not(((d == 0) & (zz == z)) | ((d == BACK) & (zz < z))))
             def _():
                 landed(unit, p_sem.at[2 * d + j])
 
@@ -298,7 +370,7 @@
                     {"y": lax.rem(y + 1, n_y)},
                 )
 
-            @pl.when((y + BACK < n_y) & (d == 0))
+            @pl.when((y + BACK < n_y) & (d == 0) & (zz >= z))
             def _():
                 send(
                     unit,
@@ -308,7 +380,7 @@
                     {"y": lax.rem(y + BACK, n_y)},
                 )
 
-            @pl.when(jnp.logical_not(mine))
+            @pl.when(seen_here(d, zz))
             def _():
                 send(unit, unit, x_snd.at[2 * d + j], x_sem.at[2 * d + j], {"x": x_mate})
                 send(unit, unit, b_snd.at[4 * d + zz], c_sem.at[4 * d + zz], {"c": c_mate})
@@ -318,7 +390,7 @@
             zz = place(other_half, j)
             unit = kv.at[c, 4 * d + zz]
 
-            @pl.when(jnp.logical_not((d == 0) & (zz == z)))
+            @pl.when(seen_here(d, zz))
             def _():
                 landed(unit, x_sem.at[2 * d + j])
                 send(unit, unit, b_snd.at[4 * d + zz], c_sem.at[4 * d + zz], {"c": c_mate})
@@ -326,7 +398,7 @@
     def complete(d):
         for zz in range(4):
 
-            @pl.when(jnp.logical_not((d == 0) & (zz == z)))
+            @pl.when(seen_here(d, zz))
             def _():
                 landed(kv.at[c_mate, 4 * d + zz], c_sem.at[4 * d + zz])
 
@@ -425,6 +497,11 @@
         sums = dot_nt(jnp.ones((8, 128), F32), squares, precision=lax.Precision.HIGHEST)
         ss_in[tp] = sums[0:1, :]
 
+    def post_squares():
+        @pl.when(own_turn < n_tp - 1)
+        def _():
+            pl.semaphore_wait(ready, n_tp - 1 - own_turn)
+
         def post(k, carry):
             send(ss_in.at[tp], ss_in.at[tp], ss_snd.at[k], ss_sem.at[tp], tp_place(k))
             return carry
@@ -453,30 +530,33 @@
 
     primary(0)
 
+    post_at = jnp.where(w == 0, 4, 1)
+
     def step(it, carry):
         d = order(it)
         after = order(it + 1)
 
+        @pl.when((it < BACK) & (after <= y))
+        def _():
+            primary(after)
+
+        @pl.when(it == 0)
+        def _():
+            row_prefixes()
+
+        @pl.when(it == 1)
+        def _():
+            carry_over()
+
+        @pl.when(it == post_at)
+        def _():
+            post_squares()
+
         @pl.when(d <= y)
         def _():
             secondary(d)
-
-        @pl.when((it < BACK) & (after <= y))
-        def _():
-            primary(after)
-
-        @pl.when(d <= y)
-        def _():
             complete(d)
             attend(d)
-
-        @pl.when(it == 0)
-        def _():
-            row_prefixes()
-
-        @pl.when(it == 1)
-        def _():
-            carry_over()
 
         return carry
 
@@ -508,23 +588,23 @@
         @pl.when(d <= y)
         def _():
             for j in range(2):
-                mine = (d == 0) & (place(half, j) == z)
+                zz = place(half, j)
 
                 @pl.when((y + 1 < n_y) & (d + 1 < BACK))
                 def _():
                     left(kv.at[c, 0], a_snd.at[2 * d + j])
 
-                @pl.when((y + BACK < n_y) & (d == 0))
+                @pl.when((y + BACK < n_y) & (d == 0) & (zz >= z))
                 def _():
                     left(kv.at[c, 0], a5_snd.at[j])
 
-                @pl.when(jnp.logical_not(mine))
+                @pl.when(seen_here(d, zz))
                 def _():
                     left(kv.at[c, 0], x_snd.at[2 * d + j])
 
             for zz in range(4):
 
-                @pl.when(jnp.logical_not((d == 0) & (zz == z)))
+                @pl.when(seen_here(d, zz))
                 def _():
                     left(kv.at[c, 0], b_snd.at[4 * d + zz])
 
@@ -542,15 +622,27 @@
     rows = BACK + 1
     unit = toks + 16
     in_vmem = pl.BlockSpec(memory_space=pltpu.VMEM)
+    in_place = pl.BlockSpec(memory_space=pl.ANY)
     lin_out, soft_out = pl.pallas_call(
         functools.partial(kernel, sizes),
         out_shape=(
             jax.ShapeDtypeStruct((2 * toks, HEAD_DIM), BF16),
             jax.ShapeDtypeStruct((2 * toks, HEAD_DIM), BF16),
         ),
-        in_specs=[in_vmem] * 10,
+        in_specs=[in_place] * 10,
         out_specs=(in_vmem, in_vmem),
         scratch_shapes=[
+            pltpu.VMEM((2 * toks, 128), BF16),
+            pltpu.VMEM((2 * toks, 128), BF16),
+            pltpu.VMEM((2 * toks, 128), BF16),
+            pltpu.VMEM((2 * toks, 128), BF16),
+            pltpu.VMEM((2, toks), F32),
+            pltpu.VMEM((2, 128), F32),
+            pltpu.VMEM((1, toks), jnp.int32),
+            pltpu.VMEM((2 * toks, 128), BF16),
+            pltpu.VMEM((KV_HEADS * toks, 128), BF16),
+            pltpu.VMEM((KV_HEADS * toks, 128), BF16),
+            dma((10,)),
             pltpu.VMEM((2, 4 * rows, unit, 128), BF16),
             pltpu.VMEM((2, KV_HEADS * toks, 128), F32),
             pltpu.VMEM((2 * toks, 128), F32),
@@ -583,6 +675,7 @@
             dma((rows,)),
             dma((4,)),
             dma((n_tp,)),
+            pltpu.SemaphoreType.REGULAR,
             dma((3,)),
             dma((2 * rows,)),
             dma((2,)),
@@ -594,7 +687,7 @@
             dma((n_tp,)),
         ],
         compiler_params=pltpu.CompilerParams(
-            collective_id=0, has_side_effects=True, vmem_limit_bytes=48 * 1024 * 1024
+            collective_id=0, has_side_effects=True, vmem_limit_bytes=56 * 1024 * 1024
         ),
     )(
         flat(lin_query),

time: 73.6 us -> 56.9 us (0.77)
  the two profiles are of different devices: /device:TPU:113 before, /device:TPU:81 now
where the time goes in v2:
time: 56.9 us; the launch traced here: 56.8 us
  Pallas kernels  53.8 us (95%)
  local copies, waits for them, and re-layouts  2.35 us (4%)
  between operations  0.65 us (1%)
    pallas_call x1, Pallas kernels, body(): pl.pallas_call(functools.partial(kernel, sizes), out_shape=(jax.ShapeDtyp...  53.8 us
    unnamed x4, local copies, waits for them, and re-layouts  2.35 us

profile of v2, /device:TPU:81, one launch (start us, length us, event | category | flops | bytes accessed | tf_op | source)
XLA Modules:
  0.0 56.8 jit_solution(4923592737943893034)
XLA Ops:
  0.6 53.8 %shard_map.113 = (bf16[512,128]{1,0:T(8,128)(2,1)}, bf16[512,128]{1,0:T(8,128)(2,1)}) custom-call(bf16[512,128]{1,0:T(8,128)(2,1)} %bitcast.15, bf16[512,128]{1,0:T(8,128)(2,1)} %bitcast.16, bf16[512,128]{1,0:T(8,128)(2,1)} %bitcast.17, bf16[512,128]{1,0:T(8,128)(2,1)} %bitcast.18, f32[2,256]{1,0:T(2,128)} %bitcast.20, f32[2,128]{1,0:T(2,128)} %gain_in.1, ...), custom_call_target="tpu_custom_call" | custom-call | tf_op jit(solution)/shard_map/pallas_call | solution.py:626
  54.4 0.0 copy-start
  54.4 1.7 %copy.14 = bf16[256,2,128]{2,1,0:T(2,128)(2,1)} copy(bf16[256,2,128]{2,1,0:T(2,128)(2,1)} %bitcast.14) | data formatting | bytes 262144
  56.1 0.0 copy-done
  56.1 0.7 %copy.15 = bf16[256,2,128]{2,1,0:T(2,128)(2,1)} copy(bf16[256,2,128]{2,1,0:T(2,128)(2,1)S(1)} %bitcast.13) | data formatting | bytes 262144
Async XLA Ops:
  54.4 1.7 %copy-start = (bf16[512,128]{1,0:T(8,128)(2,1)S(1)}, bf16[512,128]{1,0:T(8,128)(2,1)}, u32[]{:S(2)}) copy-start(bf16[512,128]{1,0:T(8,128)(2,1)} %get-tuple-element.5) | copy-start | bytes 393220

commit v3 on v2

--- a/solution.py
+++ b/solution.py
@@ -1,4 +1,5 @@
 import functools
+import math
 
 import jax
 import jax.numpy as jnp
@@ -247,12 +248,9 @@
         kv[kind, z, toks : toks + 16, :] = doc_tile
 
     doc_col = as_column(doc_row, toks)
-    dcol[...] = doc_col
-    for h in range(2):
-        dq[pl.ds(h, toks, stride=2), :] = doc_col
-    for load in loads[3:]:
+    for load in loads[3:6]:
         load.wait()
-    for source, target in ((lq, wq), (lk, wk), (lv, wv), (lg, wg)):
+    for source, target in ((lk, wk), (lv, wv)):
         target[...] = source[...].astype(F32)
 
     dec[...] = jnp.zeros_like(dec)
@@ -265,7 +263,6 @@
     ccol[...] = cum_col
     last_doc = doc_row[:, toks - 1 : toks]
     tail = (doc_col[:, :1] == last_doc).astype(F32)
-    queries = [wq[pl.ds(h, toks, stride=2), :].astype(BF16) for h in range(2)]
     keys = [wk[pl.ds(h, toks, stride=2), :] for h in range(2)]
     values = [wv[pl.ds(h, toks, stride=2), :].astype(BF16) for h in range(2)]
     decay_line = jnp.zeros((1, 128), F32)
@@ -309,6 +306,14 @@
             send(kv.at[c, z], kv.at[c, z], za_snd.at[k - 1], p_sem.at[z // 2], {"z": z2})
 
     lax.fori_loop(1, n_tp, tell_tp, 0)
+    dcol[...] = doc_col
+    for h in range(2):
+        dq[pl.ds(h, toks, stride=2), :] = doc_col
+    for load in loads[6:]:
+        load.wait()
+    for source, target in ((lq, wq), (lg, wg)):
+        target[...] = source[...].astype(F32)
+    queries = [wq[pl.ds(h, toks, stride=2), :].astype(BF16) for h in range(2)]
     visible = (s_id <= t_id) & (doc_row == doc_col[:, :1])
     for h in range(2):
         gap = cum_col[:, h : h + 1] - cum_row[h : h + 1, :]
@@ -351,39 +356,38 @@
     def seen_here(d, zz):
         return jnp.logical_not(((d == 0) & (zz >= z)) | ((d == BACK) & (zz < z)))
 
-    def primary(d):
-        for j in range(2):
-            zz = place(half, j)
-            unit = kv.at[c, 4 * d + zz]
-
-            @pl.when(jnp.logical_not(((d == 0) & (zz == z)) | ((d == BACK) & (zz < z))))
-            def _():
-                landed(unit, p_sem.at[2 * d + j])
-
-            @pl.when((y + 1 < n_y) & (d + 1 < BACK))
-            def _():
-                send(
-                    unit,
-                    kv.at[c, 4 * d + 4 + zz],
-                    a_snd.at[2 * d + j],
-                    p_sem.at[2 * d + 2 + j],
-                    {"y": lax.rem(y + 1, n_y)},
-                )
-
-            @pl.when((y + BACK < n_y) & (d == 0) & (zz >= z))
-            def _():
-                send(
-                    unit,
-                    kv.at[c, 4 * BACK + zz],
-                    a5_snd.at[j],
-                    p_sem.at[2 * BACK + j],
-                    {"y": lax.rem(y + BACK, n_y)},
-                )
-
-            @pl.when(seen_here(d, zz))
-            def _():
-                send(unit, unit, x_snd.at[2 * d + j], x_sem.at[2 * d + j], {"x": x_mate})
-                send(unit, unit, b_snd.at[4 * d + zz], c_sem.at[4 * d + zz], {"c": c_mate})
+    def primary(d, j):
+        zz = place(half, j)
+        unit = kv.at[c, 4 * d + zz]
+
+        @pl.when(jnp.logical_not(((d == 0) & (zz == z)) | ((d == BACK) & (zz < z))))
+        def _():
+            landed(unit, p_sem.at[2 * d + j])
+
+        @pl.when((y + 1 < n_y) & (d + 1 < BACK))
+        def _():
+            send(
+                unit,
+                kv.at[c, 4 * d + 4 + zz],
+                a_snd.at[2 * d + j],
+                p_sem.at[2 * d + 2 + j],
+                {"y": lax.rem(y + 1, n_y)},
+            )
+
+        @pl.when((y + BACK < n_y) & (d == 0) & (zz >= z))
+        def _():
+            send(
+                unit,
+                kv.at[c, 4 * BACK + zz],
+                a5_snd.at[j],
+                p_sem.at[2 * BACK + j],
+                {"y": lax.rem(y + BACK, n_y)},
+            )
+
+        @pl.when(seen_here(d, zz))
+        def _():
+            send(unit, unit, x_snd.at[2 * d + j], x_sem.at[2 * d + j], {"x": x_mate})
+            send(unit, unit, b_snd.at[4 * d + zz], c_sem.at[4 * d + zz], {"c": c_mate})
 
     def secondary(d):
         for j in range(2):
@@ -402,10 +406,10 @@
             def _():
                 landed(kv.at[c_mate, 4 * d + zz], c_sem.at[4 * d + zz])
 
-    score_scale = HEAD_DIM ** (-0.5)
-    rows_per = 128
-
-    def attend(d):
+    score_scale = HEAD_DIM ** (-0.5) * math.log2(math.e)
+    rows_per = toks
+
+    def attend(d, part, same_row):
         def chunk(i, carry):
             first = pl.multiple_of(i * rows_per, rows_per)
             rows = pl.ds(first, rows_per)
@@ -413,20 +417,22 @@
             query_doc = dq[rows, :][:, :1]
             line_id = lax.broadcasted_iota(jnp.int32, (rows_per, toks), 0) + first
             query_pos = lax.shift_right_logical(line_id, 1) + z * toks
-            key_id = lax.broadcasted_iota(jnp.int32, (rows_per, toks), 1)
+            ahead = query_pos - lax.broadcasted_iota(jnp.int32, (rows_per, toks), 1)
             scores = []
             for zz in range(4):
                 slot = 4 * d + zz
                 tile = kv[0, slot, toks : toks + 16, :].astype(F32)
                 key_doc = jnp.concatenate([tile[k : k + 1] for k in range(toks // 128)], axis=1)
-                seen = (key_doc == query_doc) & (key_id + (zz - 4 * d) * toks <= query_pos)
+                seen = key_doc == query_doc
+                if same_row:
+                    seen = seen & (ahead >= zz * toks)
                 score = dot_nt(query, kv[0, slot, 0:toks, :])
                 scores.append(jnp.where(seen, score, LOW))
             top = functools.reduce(jnp.maximum, scores)
             old_top = m_scr[rows, :][:, :1]
             new_top = jnp.maximum(old_top, jnp.max(top, axis=1, keepdims=True))
-            shrink = jnp.exp((old_top - new_top) * score_scale)
-            exps = [jnp.exp((score - new_top) * score_scale) for score in scores]
+            shrink = jnp.exp2((old_top - new_top) * score_scale)
+            exps = [jnp.exp2((score - new_top) * score_scale) for score in scores]
             added = jnp.sum(functools.reduce(jnp.add, exps), axis=1, keepdims=True)
             weighted = jnp.zeros((rows_per, HEAD_DIM), F32)
             for zz in range(4):
@@ -436,7 +442,8 @@
             acc[rows, :] = acc[rows, :] * shrink + weighted
             return carry
 
-        lax.fori_loop(0, 2 * toks // rows_per, chunk, 0)
+        each = toks // rows_per
+        lax.fori_loop(part * each, part * each + each, chunk, 0)
 
     def row_prefixes():
         run_state[...] = jnp.zeros_like(run_state)
@@ -528,39 +535,54 @@
     def order(it):
         return jnp.where(it == 4, 5, jnp.where(it == 5, 4, it))
 
-    primary(0)
-
+    for j in range(2):
+        primary(0, j)
     post_at = jnp.where(w == 0, 4, 1)
 
     def step(it, carry):
-        d = order(it)
-        after = order(it + 1)
-
-        @pl.when((it < BACK) & (after <= y))
-        def _():
-            primary(after)
-
-        @pl.when(it == 0)
-        def _():
-            row_prefixes()
-
-        @pl.when(it == 1)
-        def _():
-            carry_over()
-
-        @pl.when(it == post_at)
-        def _():
-            post_squares()
-
-        @pl.when(d <= y)
-        def _():
-            secondary(d)
-            complete(d)
-            attend(d)
+        past, now, after = (order(it - 1), order(it), order(it + 1))
+        has_past = (it >= 1) & (past <= y)
+        for j in range(2):
+
+            @pl.when((it < BACK) & (after <= y))
+            def _(j=j):
+                primary(after, j)
+
+            if j == 0:
+
+                @pl.when(has_past)
+                def _():
+                    complete(past)
+
+            else:
+
+                @pl.when((it <= BACK) & (now <= y))
+                def _():
+                    secondary(now)
+
+                @pl.when(it == 0)
+                def _():
+                    row_prefixes()
+
+                @pl.when(it == 1)
+                def _():
+                    carry_over()
+
+                @pl.when(it == post_at)
+                def _():
+                    post_squares()
+
+            @pl.when(has_past & (past == 0))
+            def _(j=j):
+                attend(past, j, True)
+
+            @pl.when(has_past & (past > 0))
+            def _(j=j):
+                attend(past, j, False)
 
         return carry
 
-    lax.fori_loop(0, BACK + 1, step, 0)
+    lax.fori_loop(0, BACK + 2, step, 0)
     soft_out[...] = (acc[...] / l_scr[...]).astype(BF16)
     finish_lin()
 

time: 56.9 us -> 51.8 us (0.910)
  Pallas kernels: 53.8 us -> 48.6 us
    pallas_call x1, Pallas kernels: 53.8 us -> 48.6 us  [body(): pl.pallas_call(functools.partial(kernel, sizes), out_shape=(jax.ShapeDtyp...]
where the time goes in v3:
time: 51.8 us; the launch traced here: 51.6 us
  Pallas kernels  48.6 us (94%)
  local copies, waits for them, and re-layouts  2.35 us (5%)
  between operations  0.65 us (1%)
    pallas_call x1, Pallas kernels, body(): pl.pallas_call(functools.partial(kernel, sizes), out_shape=(jax.ShapeDtyp...  48.6 us
    unnamed x4, local copies, waits for them, and re-layouts  2.35 us

profile of v3, /device:TPU:81, one launch (start us, length us, event | category | flops | bytes accessed | tf_op | source)
XLA Modules:
  0.0 51.6 jit_solution(13441021689970215507)
XLA Ops:
  0.6 48.6 %shard_map.113 = (bf16[512,128]{1,0:T(8,128)(2,1)}, bf16[512,128]{1,0:T(8,128)(2,1)}) custom-call(bf16[512,128]{1,0:T(8,128)(2,1)} %bitcast.15, bf16[512,128]{1,0:T(8,128)(2,1)} %bitcast.16, bf16[512,128]{1,0:T(8,128)(2,1)} %bitcast.17, bf16[512,128]{1,0:T(8,128)(2,1)} %bitcast.18, f32[2,256]{1,0:T(2,128)} %bitcast.20, f32[2,128]{1,0:T(2,128)} %gain_in.1, ...), custom_call_target="tpu_custom_call" | custom-call | tf_op jit(solution)/shard_map/pallas_call | solution.py:648
  49.3 0.0 copy-start
  49.3 1.7 %copy.14 = bf16[256,2,128]{2,1,0:T(2,128)(2,1)} copy(bf16[256,2,128]{2,1,0:T(2,128)(2,1)} %bitcast.14) | data formatting | bytes 262144
  51.0 0.0 copy-done
  51.0 0.7 %copy.15 = bf16[256,2,128]{2,1,0:T(2,128)(2,1)} copy(bf16[256,2,128]{2,1,0:T(2,128)(2,1)S(1)} %bitcast.13) | data formatting | bytes 262144
Async XLA Ops:
  49.3 1.7 %copy-start = (bf16[512,128]{1,0:T(8,128)(2,1)S(1)}, bf16[512,128]{1,0:T(8,128)(2,1)}, u32[]{:S(2)}) copy-start(bf16[512,128]{1,0:T(8,128)(2,1)} %get-tuple-element.5) | copy-start | bytes 393220

commit v4 on v3

--- a/solution.py
+++ b/solution.py
@@ -18,6 +18,7 @@
 F32 = jnp.float32
 BF16 = jnp.bfloat16
 BACK = 5
+DOCS = 4
 LOW = -1e30
 
 
@@ -236,16 +237,9 @@
     for load in loads[:3]:
         load.wait()
     doc_row = docs[...].astype(F32)
-    pack_row = lax.broadcasted_iota(jnp.int32, (16, 128), 0)
-    doc_tile = jnp.zeros((16, 128), F32)
-    for k in range(toks // 128):
-        piece = jnp.broadcast_to(doc_row[:, 128 * k : 128 * (k + 1)], (16, 128))
-        doc_tile = jnp.where(pack_row == k, piece, doc_tile)
-    doc_tile = doc_tile.astype(BF16)
     for kind, source in ((0, sk), (1, sv)):
         wide8[kind] = source[...].astype(F32)
-        kv[kind, z, 0:toks, :] = wide8[kind, pl.ds(head, toks, stride=KV_HEADS), :].astype(BF16)
-        kv[kind, z, toks : toks + 16, :] = doc_tile
+        kv[kind, z] = wide8[kind, pl.ds(head, toks, stride=KV_HEADS), :].astype(BF16)
 
     doc_col = as_column(doc_row, toks)
     for load in loads[3:6]:
@@ -275,6 +269,9 @@
             s_out[q, 32 * h : 32 * h + 32, :] = state[32 * q : 32 * q + 32, :]
         decay_line = jnp.where(lane == h, end, decay_line)
     decay_line = jnp.where(lane == 2, last_doc, decay_line)
+    for v in range(DOCS):
+        count = jnp.sum((doc_row == v).astype(F32), axis=1, keepdims=True)
+        decay_line = jnp.where(lane == 3 + v, count, decay_line)
     scalars = three_parts(decay_line)
     for q in range(4):
         s_out[q, 64:80, :] = scalars
@@ -285,11 +282,11 @@
 
             @pl.when((zz > z) & jnp.logical_not(in_half & (c == kind)))
             def _(zz=zz, kind=kind):
-                kv[kind, zz] = jnp.full(kv.shape[2:], -1.0, BF16)
+                kv[kind, zz] = jnp.zeros(kv.shape[2:], BF16)
 
             @pl.when((zz < z) & (y >= BACK))
             def _(zz=zz, kind=kind):
-                kv[kind, 4 * BACK + zz] = jnp.full(kv.shape[2:], -1.0, BF16)
+                kv[kind, 4 * BACK + zz] = jnp.zeros(kv.shape[2:], BF16)
 
     early_mates = c + jnp.where(turn(w, x_mate, c) < own_turn, 1, 0)
     pl.semaphore_wait(barrier, (n_z - 1) + (n_y - 1) + 2 + own_turn - early_mates)
@@ -414,19 +411,18 @@
             first = pl.multiple_of(i * rows_per, rows_per)
             rows = pl.ds(first, rows_per)
             query = sq[rows, :]
-            query_doc = dq[rows, :][:, :1]
+            key_id = lax.broadcasted_iota(jnp.int32, (rows_per, toks), 1)
+            inside = key_id.astype(F32) - dq[rows, :][:, :1]
             line_id = lax.broadcasted_iota(jnp.int32, (rows_per, toks), 0) + first
             query_pos = lax.shift_right_logical(line_id, 1) + z * toks
-            ahead = query_pos - lax.broadcasted_iota(jnp.int32, (rows_per, toks), 1)
+            ahead = query_pos - key_id
             scores = []
             for zz in range(4):
                 slot = 4 * d + zz
-                tile = kv[0, slot, toks : toks + 16, :].astype(F32)
-                key_doc = jnp.concatenate([tile[k : k + 1] for k in range(toks // 128)], axis=1)
-                seen = key_doc == query_doc
+                seen = inside >= ((4 * d - zz) * toks).astype(F32)
                 if same_row:
                     seen = seen & (ahead >= zz * toks)
-                score = dot_nt(query, kv[0, slot, 0:toks, :])
+                score = dot_nt(query, kv[0, slot])
                 scores.append(jnp.where(seen, score, LOW))
             top = functools.reduce(jnp.maximum, scores)
             old_top = m_scr[rows, :][:, :1]
@@ -436,7 +432,7 @@
             added = jnp.sum(functools.reduce(jnp.add, exps), axis=1, keepdims=True)
             weighted = jnp.zeros((rows_per, HEAD_DIM), F32)
             for zz in range(4):
-                weighted = weighted + dot_nn(exps[zz].astype(BF16), kv[1, 4 * d + zz, 0:toks, :])
+                weighted = weighted + dot_nn(exps[zz].astype(BF16), kv[1, 4 * d + zz])
             m_scr[rows, :] = jnp.broadcast_to(new_top, (rows_per, 128))
             l_scr[rows, :] = l_scr[rows, :] * shrink + added
             acc[rows, :] = acc[rows, :] * shrink + weighted
@@ -478,6 +474,14 @@
                         part = part * weight_of(j + 1, k - 1, h, ends[j])
                     prior = prior + part
                 p_out[k, rows, :] = prior.astype(BF16)
+        began = jnp.zeros((1, 1), F32)
+        starts = jnp.zeros(dq.shape, F32)
+        for v in range(DOCS):
+            earlier = run_decay[0:1, 3 + v : 4 + v]
+            first = jnp.where(earlier > 0, -earlier, began)
+            starts = jnp.where(dq[...] == v, first, starts)
+            began = began + total_line[:, 3 + v : 4 + v]
+        dq[...] = starts
         own_doc = before
         for k in range(1, 4):
             own_doc = jnp.where(z == k, ends[k - 1], own_doc)
@@ -526,10 +530,7 @@
         inv = lax.rsqrt(total / (n_tp * 2 * HEAD_DIM) + 1e-06)
         inv_col = as_column(inv, toks)
         for h in range(2):
-            gate = wg[pl.ds(h, toks, stride=2), :]
-            wo[pl.ds(h, toks, stride=2), :] = (
-                mix[h] * inv_col * gain[h : h + 1, :] * jax.nn.sigmoid(gate)
-            )
+            wo[pl.ds(h, toks, stride=2), :] = mix[h] * inv_col
         lin_out[...] = wo[...].astype(BF16)
 
     def order(it):
@@ -584,7 +585,9 @@
 
     lax.fori_loop(0, BACK + 2, step, 0)
     soft_out[...] = (acc[...] / l_scr[...]).astype(BF16)
-    finish_lin()
+    for h in range(2):
+        gate = wg[pl.ds(h, toks, stride=2), :]
+        mix[h] = mix[h] * gain[h : h + 1, :] * jax.nn.sigmoid(gate)
 
     for k in range(n_z - 1):
         left(s_out.at[0], s_snd.at[k])
@@ -633,6 +636,18 @@
         return carry
 
     lax.fori_loop(0, BACK + 1, row_sent, 0)
+    finish_lin()
+
+
+def hand_over(lin, soft, lin_out, soft_out, sem):
+    copies = [
+        pltpu.make_async_copy(lin, lin_out, sem.at[0]),
+        pltpu.make_async_copy(soft, soft_out, sem.at[1]),
+    ]
+    for copy in copies:
+        copy.start()
+    for copy in copies:
+        copy.wait()
 
 
 def body(sizes, lin_query, lin_key, lin_value, lin_gate, log_decay, norm_gain, doc_ids,
@@ -642,14 +657,13 @@
     flat = lambda a: a.reshape(-1, HEAD_DIM)
     dma = pltpu.SemaphoreType.DMA
     rows = BACK + 1
-    unit = toks + 16
     in_vmem = pl.BlockSpec(memory_space=pltpu.VMEM)
     in_place = pl.BlockSpec(memory_space=pl.ANY)
     lin_out, soft_out = pl.pallas_call(
         functools.partial(kernel, sizes),
         out_shape=(
-            jax.ShapeDtypeStruct((2 * toks, HEAD_DIM), BF16),
-            jax.ShapeDtypeStruct((2 * toks, HEAD_DIM), BF16),
+            pltpu.VMEM((2 * toks, HEAD_DIM), BF16),
+            pltpu.VMEM((2 * toks, HEAD_DIM), BF16),
         ),
         in_specs=[in_place] * 10,
         out_specs=(in_vmem, in_vmem),
@@ -665,7 +679,7 @@
             pltpu.VMEM((KV_HEADS * toks, 128), BF16),
             pltpu.VMEM((KV_HEADS * toks, 128), BF16),
             dma((10,)),
-            pltpu.VMEM((2, 4 * rows, unit, 128), BF16),
+            pltpu.VMEM((2, 4 * rows, toks, 128), BF16),
             pltpu.VMEM((2, KV_HEADS * toks, 128), F32),
             pltpu.VMEM((2 * toks, 128), F32),
             pltpu.VMEM((2 * toks, 128), F32),
@@ -723,6 +737,17 @@
         flat(soft_key),
         flat(soft_value),
     )
+    lin_out, soft_out = pl.pallas_call(
+        hand_over,
+        out_shape=(
+            jax.ShapeDtypeStruct((2 * toks, HEAD_DIM), BF16),
+            jax.ShapeDtypeStruct((2 * toks, HEAD_DIM), BF16),
+        ),
+        in_specs=[in_vmem] * 2,
+        out_specs=(in_place, in_place),
+        scratch_shapes=[dma((2,))],
+        compiler_params=pltpu.CompilerParams(vmem_limit_bytes=8 * 1024 * 1024),
+    )(lin_out, soft_out)
     return lin_out.reshape(toks, 2, HEAD_DIM), soft_out.reshape(toks, 2, HEAD_DIM)
 
 

time: 51.8 us -> 48.5 us (0.936)
  local copies, waits for them, and re-layouts: 2.35 us -> 0 us
  Pallas kernels: 48.6 us -> 47.7 us
    unnamed x4 -> x0, local copies, waits for them, and re-layouts: 2.35 us -> none
    pallas_call x1 -> x2, Pallas kernels: 48.6 us -> 47.7 us  [the longest x1 47 us: body(): pl.pallas_call(functools.partial(kernel, sizes), out_shape=(pltpu.VMEM((2...]
where the time goes in v4:
time: 48.5 us; the launch traced here: 48.3 us
  Pallas kernels  47.7 us (98%)
  between operations  0.64 us (1%)
    pallas_call x1, Pallas kernels, body(): pl.pallas_call(functools.partial(kernel, sizes), out_shape=(pltpu.VMEM((2...  47 us

profile of v4, /device:TPU:81, one launch (start us, length us, event | category | flops | bytes accessed | tf_op | source)
XLA Modules:
  0.0 48.3 jit_solution(6761724186969562069)
XLA Ops:
  0.6 47.0 %shard_map.113 = (bf16[512,128]{1,0:T(8,128)(2,1)S(1)}, bf16[512,128]{1,0:T(8,128)(2,1)S(1)}) custom-call(bf16[512,128]{1,0:T(8,128)(2,1)} %bitcast.13, bf16[512,128]{1,0:T(8,128)(2,1)} %bitcast.14, bf16[512,128]{1,0:T(8,128)(2,1)} %bitcast.15, bf16[512,128]{1,0:T(8,128)(2,1)} %bitcast.16, f32[2,256]{1,0:T(2,128)} %bitcast.18, f32[2,128]{1,0:T(2,128)} %gain_in.1, ...), custom_call_target="tpu_custom_call" | custom-call | tf_op jit(solution)/shard_map/pallas_call | solution.py:662
  47.6 0.7 %shard_map.114 = (bf16[512,128]{1,0:T(8,128)(2,1)}, bf16[512,128]{1,0:T(8,128)(2,1)}) custom-call(bf16[512,128]{1,0:T(8,128)(2,1)S(1)} %get-tuple-element.6.lin, bf16[512,128]{1,0:T(8,128)(2,1)S(1)} %get-tuple-element.7.soft), custom_call_target="tpu_custom_call" | custom-call | tf_op jit(solution)/shard_map/pallas_call | solution.py:740

commit v5 on v4

--- a/solution.py
+++ b/solution.py
@@ -141,9 +141,13 @@
     c_mate = 1 - c
     head = (tp * 2) // (HEADS // KV_HEADS)
 
+    n_xc = n_x * n_c
+
     def tp_place(k):
-        t2 = lax.rem(tp + k, n_tp)
-        return {"w": t2 // (n_x * n_c), "x": lax.rem(t2 // n_c, n_x), "c": lax.rem(t2, n_c)}
+        away = k <= n_tp - n_xc
+        w2 = lax.rem(w + jnp.where(away, 1, 0), n_w)
+        xc2 = lax.rem(x * n_c + c + k - jnp.where(away, 1, n_tp - n_xc), n_xc)
+        return {"w": w2, "x": xc2 // n_c, "c": lax.rem(xc2, n_c)}
 
     def turn(w_, x_, c_):
         apart = jnp.minimum(x_, n_x - x_)
@@ -153,23 +157,17 @@
     own_turn = turn(w, x, c)
     barrier = pltpu.get_barrier_semaphore()
 
-    def greet_tp(k, carry):
-        other = tp_place(k)
-        near = ((other["x"] == x) | ((other["x"] == x_mate) & (other["c"] == c))) & (other["w"] == w)
-
-        @pl.when(near | (turn(other["w"], other["x"], other["c"]) > own_turn))
-        def _():
-            pl.semaphore_signal(barrier, inc=1, device_id=other, device_id_type=MESH)
-
+    def at_turn(t):
+        step = lax.rem(t, n_xc) // n_c
+        x2 = jnp.where(lax.rem(step, 2) == 1, (step + 1) // 2, n_x - step // 2)
+        return {"w": t // n_xc, "x": lax.rem(x2, n_x), "c": lax.rem(t, n_c)}
+
+    def greet_tp(t, carry):
+        pl.semaphore_signal(barrier, inc=1, device_id=at_turn(t), device_id_type=MESH)
         return carry
 
-    def tell_tp(k, carry):
-        other = tp_place(k)
-
-        @pl.when(turn(other["w"], other["x"], other["c"]) < own_turn)
-        def _():
-            pl.semaphore_signal(ready, inc=1, device_id=other, device_id_type=MESH)
-
+    def tell_tp(t, carry):
+        pl.semaphore_signal(ready, inc=1, device_id=at_turn(t), device_id_type=MESH)
         return carry
 
     def greet_y(k, carry):
@@ -182,12 +180,12 @@
         pltpu.make_async_copy(source, target, in_sem.at[k])
         for k, (source, target) in enumerate(
             (
-                (sk_in, sk),
-                (sv_in, sv),
                 (docs_in, docs),
                 (ld_in, ld),
                 (lk_in, lk),
                 (lv_in, lv),
+                (sk_in, sk),
+                (sv_in, sv),
                 (lq_in, lq),
                 (lg_in, lg),
                 (sq_in, sq),
@@ -202,7 +200,16 @@
             barrier, inc=1, device_id={"z": lax.rem(z + k, n_z)}, device_id_type=MESH
         )
     lax.fori_loop(1, n_y, greet_y, 0)
-    lax.fori_loop(1, n_tp, greet_tp, 0)
+
+    @pl.when(c == 1)
+    def _():
+        pl.semaphore_signal(barrier, inc=1, device_id={"c": c_mate}, device_id_type=MESH)
+
+    @pl.when(turn(w, x_mate, c) < own_turn)
+    def _():
+        pl.semaphore_signal(barrier, inc=1, device_id={"x": x_mate}, device_id_type=MESH)
+
+    lax.fori_loop(own_turn + 1, n_tp, greet_tp, 0)
 
     def send(src, dst, send_sem, recv_sem, device):
         pltpu.make_async_remote_copy(
@@ -234,16 +241,10 @@
             device_id_type=MESH,
         ).wait_send()
 
-    for load in loads[:3]:
+    for load in loads[:4]:
         load.wait()
     doc_row = docs[...].astype(F32)
-    for kind, source in ((0, sk), (1, sv)):
-        wide8[kind] = source[...].astype(F32)
-        kv[kind, z] = wide8[kind, pl.ds(head, toks, stride=KV_HEADS), :].astype(BF16)
-
     doc_col = as_column(doc_row, toks)
-    for load in loads[3:6]:
-        load.wait()
     for source, target in ((lk, wk), (lv, wv)):
         target[...] = source[...].astype(F32)
 
@@ -276,6 +277,27 @@
     for q in range(4):
         s_out[q, 64:80, :] = scalars
     s_in[z] = s_out[z]
+    early_mates = c + jnp.where(turn(w, x_mate, c) < own_turn, 1, 0)
+
+    def greeted_and_sent():
+        pl.semaphore_wait(barrier, (n_z - 1) + (n_y - 1) + 2 + own_turn - early_mates)
+
+        for k in range(1, n_z):
+            z2 = lax.rem(z + k, n_z)
+            send(s_out.at[z2], s_in.at[z], s_snd.at[k - 1], s_sem.at[z], {"z": z2})
+
+    late = w == 1
+
+    @pl.when(late)
+    def _():
+        greeted_and_sent()
+
+    for load in loads[4:6]:
+        load.wait()
+    for kind, source in ((0, sk), (1, sv)):
+        wide8[kind] = source[...].astype(F32)
+        kv[kind, z] = wide8[kind, pl.ds(head, toks, stride=KV_HEADS), :].astype(BF16)
+
     for zz in range(4):
         in_half = ((zz == 0) or (zz == 3)) == (half == 0)
         for kind in range(2):
@@ -288,12 +310,10 @@
             def _(zz=zz, kind=kind):
                 kv[kind, 4 * BACK + zz] = jnp.zeros(kv.shape[2:], BF16)
 
-    early_mates = c + jnp.where(turn(w, x_mate, c) < own_turn, 1, 0)
-    pl.semaphore_wait(barrier, (n_z - 1) + (n_y - 1) + 2 + own_turn - early_mates)
-
-    for k in range(1, n_z):
-        z2 = lax.rem(z + k, n_z)
-        send(s_out.at[z2], s_in.at[z], s_snd.at[k - 1], s_sem.at[z], {"z": z2})
+    @pl.when(jnp.logical_not(late))
+    def _():
+        greeted_and_sent()
+
     owner = ((z == 0) | (z == 3)) == (half == 0)
 
     @pl.when(owner)
@@ -302,7 +322,7 @@
             z2 = lax.rem(z + jnp.where(z < 2, n_z - k, k), n_z)
             send(kv.at[c, z], kv.at[c, z], za_snd.at[k - 1], p_sem.at[z // 2], {"z": z2})
 
-    lax.fori_loop(1, n_tp, tell_tp, 0)
+    lax.fori_loop(0, own_turn, tell_tp, 0)
     dcol[...] = doc_col
     for h in range(2):
         dq[pl.ds(h, toks, stride=2), :] = doc_col
@@ -536,13 +556,52 @@
     def order(it):
         return jnp.where(it == 4, 5, jnp.where(it == 5, 4, it))
 
+    @pl.when(y == 0)
+    def _():
+        row_prefixes()
+
     for j in range(2):
         primary(0, j)
-    post_at = jnp.where(w == 0, 4, 1)
+
+    def row_sent(it, carry):
+        d = order(it)
+
+        @pl.when(d <= y)
+        def _():
+            for j in range(2):
+                zz = place(half, j)
+
+                @pl.when((y + 1 < n_y) & (d + 1 < BACK))
+                def _():
+                    left(kv.at[c, 0], a_snd.at[2 * d + j])
+
+                @pl.when((y + BACK < n_y) & (d == 0) & (zz >= z))
+                def _():
+                    left(kv.at[c, 0], a5_snd.at[j])
+
+                @pl.when(seen_here(d, zz))
+                def _():
+                    left(kv.at[c, 0], x_snd.at[2 * d + j])
+
+            for zz in range(4):
+
+                @pl.when(seen_here(d, zz))
+                def _():
+                    left(kv.at[c, 0], b_snd.at[4 * d + zz])
+
+        return carry
 
     def step(it, carry):
         past, now, after = (order(it - 1), order(it), order(it + 1))
         has_past = (it >= 1) & (past <= y)
+        @pl.when(late & (it == 1))
+        def _():
+            carry_over()
+
+        @pl.when(late & (it == 1))
+        def _():
+            post_squares()
+
         for j in range(2):
 
             @pl.when((it < BACK) & (after <= y))
@@ -551,6 +610,10 @@
 
             if j == 0:
 
+                @pl.when(late & (it == 0) & (y > 0))
+                def _():
+                    row_prefixes()
+
                 @pl.when(has_past)
                 def _():
                     complete(past)
@@ -561,15 +624,15 @@
                 def _():
                     secondary(now)
 
-                @pl.when(it == 0)
+                @pl.when(jnp.logical_not(late) & (it == 0) & (y > 0))
                 def _():
                     row_prefixes()
 
-                @pl.when(it == 1)
+                @pl.when(jnp.logical_not(late) & (it == 1))
                 def _():
                     carry_over()
 
-                @pl.when(it == post_at)
+                @pl.when(jnp.logical_not(late) & (it == 4))
                 def _():
                     post_squares()
 
@@ -581,13 +644,20 @@
             def _(j=j):
                 attend(past, j, False)
 
+        @pl.when(it == BACK - 1)
+        def _():
+            for h in range(2):
+                gate = wg[pl.ds(h, toks, stride=2), :]
+                mix[h] = mix[h] * gain[h : h + 1, :] * jax.nn.sigmoid(gate)
+
+        @pl.when(it == BACK)
+        def _():
+            lax.fori_loop(0, BACK, row_sent, 0)
+
         return carry
 
     lax.fori_loop(0, BACK + 2, step, 0)
     soft_out[...] = (acc[...] / l_scr[...]).astype(BF16)
-    for h in range(2):
-        gate = wg[pl.ds(h, toks, stride=2), :]
-        mix[h] = mix[h] * gain[h : h + 1, :] * jax.nn.sigmoid(gate)
 
     for k in range(n_z - 1):
         left(s_out.at[0], s_snd.at[k])
@@ -609,33 +679,7 @@
 
     lax.fori_loop(1, n_tp, sent, 0)
 
-    def row_sent(d, carry):
-        @pl.when(d <= y)
-        def _():
-            for j in range(2):
-                zz = place(half, j)
-
-                @pl.when((y + 1 < n_y) & (d + 1 < BACK))
-                def _():
-                    left(kv.at[c, 0], a_snd.at[2 * d + j])
-
-                @pl.when((y + BACK < n_y) & (d == 0) & (zz >= z))
-                def _():
-                    left(kv.at[c, 0], a5_snd.at[j])
-
-                @pl.when(seen_here(d, zz))
-                def _():
-                    left(kv.at[c, 0], x_snd.at[2 * d + j])
-
-            for zz in range(4):
-
-                @pl.when(seen_here(d, zz))
-                def _():
-                    left(kv.at[c, 0], b_snd.at[4 * d + zz])
-
-        return carry
-
-    lax.fori_loop(0, BACK + 1, row_sent, 0)
+    row_sent(BACK, 0)
     finish_lin()
 
 

time: 48.5 us -> 48.3 us (level)
  no operation moved by 1% of the time
where the time goes in v5:
time: 48.3 us; the launch traced here: 48.1 us
  Pallas kernels  47.5 us (98%)
  between operations  0.64 us (1%)
    pallas_call x1, Pallas kernels, body(): pl.pallas_call(functools.partial(kernel, sizes), out_shape=(pltpu.VMEM((2...  46.8 us

profile of v5, /device:TPU:81, one launch (start us, length us, event | category | flops | bytes accessed | tf_op | source)
XLA Modules:
  0.0 48.1 jit_solution(9916762757586074469)
XLA Ops:
  0.6 46.8 %shard_map.113 = (bf16[512,128]{1,0:T(8,128)(2,1)S(1)}, bf16[512,128]{1,0:T(8,128)(2,1)S(1)}) custom-call(bf16[512,128]{1,0:T(8,128)(2,1)} %bitcast.13, bf16[512,128]{1,0:T(8,128)(2,1)} %bitcast.14, bf16[512,128]{1,0:T(8,128)(2,1)} %bitcast.15, bf16[512,128]{1,0:T(8,128)(2,1)} %bitcast.16, f32[2,256]{1,0:T(2,128)} %bitcast.18, f32[2,128]{1,0:T(2,128)} %gain_in.1, ...), custom_call_target="tpu_custom_call" | custom-call | tf_op jit(solution)/shard_map/pallas_call | solution.py:706
  47.4 0.7 %shard_map.114 = (bf16[512,128]{1,0:T(8,128)(2,1)}, bf16[512,128]{1,0:T(8,128)(2,1)}) custom-call(bf16[512,128]{1,0:T(8,128)(2,1)S(1)} %get-tuple-element.6.lin, bf16[512,128]{1,0:T(8,128)(2,1)S(1)} %get-tuple-element.7.soft), custom_call_target="tpu_custom_call" | custom-call | tf_op jit(solution)/shard_map/pallas_call | solution.py:784

commit v6 on v5

--- a/solution.py
+++ b/solution.py
@@ -416,8 +416,8 @@
                 landed(unit, x_sem.at[2 * d + j])
                 send(unit, unit, b_snd.at[4 * d + zz], c_sem.at[4 * d + zz], {"c": c_mate})
 
-    def complete(d):
-        for zz in range(4):
+    def complete(d, blocks):
+        for zz in blocks:
 
             @pl.when(seen_here(d, zz))
             def _():
@@ -426,7 +426,7 @@
     score_scale = HEAD_DIM ** (-0.5) * math.log2(math.e)
     rows_per = toks
 
-    def attend(d, part, same_row):
+    def attend(d, part, same_row, blocks):
         def chunk(i, carry):
             first = pl.multiple_of(i * rows_per, rows_per)
             rows = pl.ds(first, rows_per)
@@ -437,7 +437,7 @@
             query_pos = lax.shift_right_logical(line_id, 1) + z * toks
             ahead = query_pos - key_id
             scores = []
-            for zz in range(4):
+            for zz in blocks:
                 slot = 4 * d + zz
                 seen = inside >= ((4 * d - zz) * toks).astype(F32)
                 if same_row:
@@ -451,8 +451,8 @@
             exps = [jnp.exp2((score - new_top) * score_scale) for score in scores]
             added = jnp.sum(functools.reduce(jnp.add, exps), axis=1, keepdims=True)
             weighted = jnp.zeros((rows_per, HEAD_DIM), F32)
-            for zz in range(4):
-                weighted = weighted + dot_nn(exps[zz].astype(BF16), kv[1, 4 * d + zz])
+            for part_exp, zz in zip(exps, blocks):
+                weighted = weighted + dot_nn(part_exp.astype(BF16), kv[1, 4 * d + zz])
             m_scr[rows, :] = jnp.broadcast_to(new_top, (rows_per, 128))
             l_scr[rows, :] = l_scr[rows, :] * shrink + added
             acc[rows, :] = acc[rows, :] * shrink + weighted
@@ -594,6 +594,10 @@
     def step(it, carry):
         past, now, after = (order(it - 1), order(it), order(it + 1))
         has_past = (it >= 1) & (past <= y)
+        @pl.when(late & (it == 0) & (y > 0))
+        def _():
+            row_prefixes()
+
         @pl.when(late & (it == 1))
         def _():
             carry_over()
@@ -610,15 +614,22 @@
 
             if j == 0:
 
-                @pl.when(late & (it == 0) & (y > 0))
-                def _():
-                    row_prefixes()
-
-                @pl.when(has_past)
-                def _():
-                    complete(past)
+                @pl.when(has_past & (it <= BACK))
+                def _():
+                    complete(past, range(4))
+
+                @pl.when(has_past & (it > BACK))
+                def _():
+                    complete(past, [place(other_half, k) for k in range(2)])
 
             else:
+
+                @pl.when((it == BACK) & (now <= y))
+                def _():
+                    own = [place(half, k) for k in range(2)]
+                    complete(now, own)
+                    for part in range(2):
+                        attend(now, part, False, own)
 
                 @pl.when((it <= BACK) & (now <= y))
                 def _():
@@ -638,11 +649,15 @@
 
             @pl.when(has_past & (past == 0))
             def _(j=j):
-                attend(past, j, True)
-
-            @pl.when(has_past & (past > 0))
+                attend(past, j, True, range(4))
+
+            @pl.when(has_past & (past > 0) & (it <= BACK))
             def _(j=j):
-                attend(past, j, False)
+                attend(past, j, False, range(4))
+
+            @pl.when(has_past & (it > BACK))
+            def _(j=j):
+                attend(past, j, False, [place(other_half, k) for k in range(2)])
 
         @pl.when(it == BACK - 1)
         def _():

time: 48.3 us -> 48.3 us (level)
  no operation moved by 1% of the time
where the time goes in v6:
time: 48.3 us; the launch traced here: 48.2 us
  Pallas kernels  47.5 us (98%)
  between operations  0.64 us (1%)
    pallas_call x1, Pallas kernels, body(): pl.pallas_call(functools.partial(kernel, sizes), out_shape=(pltpu.VMEM((2...  46.8 us

profile of v6, /device:TPU:81, one launch (start us, length us, event | category | flops | bytes accessed | tf_op | source)
XLA Modules:
  0.0 48.2 jit_solution(10850325943678261062)
XLA Ops:
  0.6 46.8 %shard_map.113 = (bf16[512,128]{1,0:T(8,128)(2,1)S(1)}, bf16[512,128]{1,0:T(8,128)(2,1)S(1)}) custom-call(bf16[512,128]{1,0:T(8,128)(2,1)} %bitcast.13, bf16[512,128]{1,0:T(8,128)(2,1)} %bitcast.14, bf16[512,128]{1,0:T(8,128)(2,1)} %bitcast.15, bf16[512,128]{1,0:T(8,128)(2,1)} %bitcast.16, f32[2,256]{1,0:T(2,128)} %bitcast.18, f32[2,128]{1,0:T(2,128)} %gain_in.1, ...), custom_call_target="tpu_custom_call" | custom-call | tf_op jit(solution)/shard_map/pallas_call | solution.py:721
  47.5 0.7 %shard_map.114 = (bf16[512,128]{1,0:T(8,128)(2,1)}, bf16[512,128]{1,0:T(8,128)(2,1)}) custom-call(bf16[512,128]{1,0:T(8,128)(2,1)S(1)} %get-tuple-element.6.lin, bf16[512,128]{1,0:T(8,128)(2,1)S(1)} %get-tuple-element.7.soft), custom_call_target="tpu_custom_call" | custom-call | tf_op jit(solution)/shard_map/pallas_call | solution.py:799
